TPU v7x, 256 devices: a whole 4x4x8 slice. The times are simulated.
256 devices in a mesh: gx: 8 (over x, core), gy: 4 (over y), gz: 8 (over z).
Axes of the slice: x: 4, y: 4, z: 8, core: 2. Of those that a mesh axis runs over, the one named last changes fastest.
Arguments:
- right_side: float32 [3, 64, 32, 64, 128], P(None, 'gx', 'gy', 'gz'), may hold values from -24 to 24
- stiffness: float32 [3, 64, 32, 64], P(None, 'gx', 'gy', 'gz'), may hold values from 0.25 to 4
- local_factor: bfloat16 [8, 4, 8, 2048, 2048], P('gx', 'gy', 'gz'), as said below
- basis: bfloat16 [8, 4, 8, 64, 1536], P('gx', 'gy', 'gz'), may hold values from -0.3125 to 0.3125
- coarse_map: int32 [8, 4, 8, 64], P('gx', 'gy', 'gz'), may hold values from 0 to 63, each once within a row
- margin_index: int32 [8, 4, 8, 512], P('gx', 'gy', 'gz'), may hold values from 0 to 1151, as said below
- coarse_inverse: bfloat16 [16384, 16384], P(('gx', 'gy', 'gz')), as said below
Outputs:
- solution: float32 [3, 64, 32, 64, 128], P(None, 'gx', 'gy', 'gz')
- residual_ratio: float32 [128], replicated
Inputs may be any that keep to these rules, and one draw needn't show every extreme that they name: `local_factor`: each subdomain's factor is zero above its diagonal. coarse_inverse is symmetric. `margin_index`: within each subdomain the 512 entries are distinct and increasing. `coarse_map`: each subdomain's entries are a permutation of 0 to 63.
All inputs are finite; a program needn't handle non-finite values.
Results may differ from a plain program's by a relative error of at most 0.0055.
Values may be sent and summed in bfloat16 or wider, within the bound.
No kernel may reach another device: no remote copies, remote signals or barrier semaphores. Data moves between devices by JAX's collectives and lax.ppermute only.
A program may use at most 64 MiB of HBM per device.

v0:
```python
import functools

import jax
import jax.numpy as jnp
from jax import lax
from jax.experimental import pallas as pl
from jax.experimental.pallas import tpu as pltpu
from jax.sharding import Mesh
from jax.sharding import PartitionSpec as P


X, C, Z = "gx_0", "gx_1", "gz"
GX, Y = (X, C), ("gy_0", "gy_1")
GX_GY_GZ = (*GX, *Y, Z)

EPSILON = 1e-06
SCALE = 2.0**-14
TILE = 256
SOME = 128


def shift(value, axis, step):
    count = lax.axis_size(axis)
    return lax.ppermute(value, axis, [(i, (i + step) % count) for i in range(count)])


def ends(blocks, dim):
    length, lanes = blocks.shape[dim], blocks.shape[-1]
    first = lax.slice_in_dim(blocks, 0, 1, axis=dim).reshape(-1, lanes)
    last = lax.slice_in_dim(blocks, length - 1, length, axis=dim).reshape(-1, lanes)
    return first, last


def swap_faces(blocks):
    first, last = ends(blocks, 1)
    lower = lax.axis_index(C) == 0
    inside = shift(jnp.where(lower, last, first), C, 1)
    peers = lax.axis_size(GX)
    up = [(i, i + 1) for i in range(1, peers - 1, 2)]
    across = lax.ppermute(
        jnp.where(lower, first, last), GX, up + [(b, a) for a, b in up]
    )
    return inside, across


def halo(blocks):
    inside, across = swap_faces(blocks)
    lower = lax.axis_index(C) == 0
    faces = [jnp.where(lower, across, inside), jnp.where(lower, inside, across)]
    for axis, dim in ((Y, 2), (Z, 3)):
        first, last = ends(blocks, dim)
        up = [(i, i + 1) for i in range(lax.axis_size(axis) - 1)]
        faces.append(lax.ppermute(last, axis, up))
        faces.append(lax.ppermute(first, axis, [(b, a) for a, b in up]))
    return faces


def inner(left, right):
    return jnp.sum(left * right, axis=(0, 1, 2, 3))


def weights(gram):
    raw_raw, one_raw, one_one, two_raw, two_one, two_two = (gram[i] for i in range(6))
    start_square = raw_raw / (SCALE * SCALE) + EPSILON
    start_norm = jnp.sqrt(start_square)
    size = start_norm * SCALE
    square = size * size
    kept = raw_raw / square
    along_one = one_raw / square
    rest_one = one_one / square - along_one * along_one * (2.0 - kept)
    rest_one = jnp.maximum(rest_one, 0.0) + EPSILON
    norm_two = jnp.sqrt(rest_one)
    kept_two = (rest_one - EPSILON) / rest_one
    shared = along_one * (1.0 - kept) / norm_two
    cross_two = (two_raw - along_one * one_raw) / (square * norm_two)
    along_two = (
        (two_one - along_one * two_raw) - along_one * (one_one - along_one * one_raw)
    ) / (square * rest_one)
    image_square = (two_two - along_one * (2.0 * two_one - along_one * one_one)) / (
        square * rest_one
    )
    rest_two = (
        image_square
        - cross_two * cross_two * (2.0 - kept)
        - along_two * along_two * (2.0 - kept_two)
        + 2.0 * cross_two * along_two * shared
    )
    norm_three = jnp.sqrt(jnp.maximum(rest_two, 0.0) + EPSILON)
    radius_one = jnp.sqrt(along_one * along_one + norm_two * norm_two)
    cosine_one = along_one / radius_one
    sine_one = norm_two / radius_one
    turned_one = cosine_one * cross_two + sine_one * along_two
    turned_two = cosine_one * along_two - sine_one * cross_two
    radius_two = jnp.sqrt(turned_two * turned_two + norm_three * norm_three)
    cosine_two = turned_two / radius_two
    sine_two = norm_three / radius_two
    coef_two = -cosine_two * sine_one * start_norm / radius_two
    coef_one = (cosine_one * start_norm - turned_one * coef_two) / radius_one
    weight_two = coef_two / (size * norm_two)
    weight_one = coef_one / size - along_one * weight_two
    return (weight_one, weight_two, sine_one * sine_two)


def local_kernel(place, order, own, *rest):
    faces, (factor, out, held, stacked, front, ring, done) = rest[:6], rest[6:]
    size = stacked.shape[0]
    own_count = own.shape[0]
    tiles = size // TILE
    half = size // 2

    def rows(i):
        return pl.ds(pl.multiple_of(i * TILE, TILE), TILE)

    def copy(i, width):
        return pltpu.make_async_copy(
            factor.at[rows(i), pl.ds(0, width)], held.at[rows(i), pl.ds(0, width)], done.at[i]
        )

    for i in range(tiles):
        copy(i, half if i < tiles // 2 else size).start()
    stacked[:own_count] = own[...]
    inside, across, y_low, y_high, z_low, z_high = faces
    per_part = inside.shape[0] // 3
    lower = place[0] == 0
    for part in range(3):

        def layer(face):
            skip = face.shape[0] - inside.shape[0]
            return face[pl.ds(skip + part * per_part, per_part)]

        def put(k, value):
            ring[pl.ds((part * 6 + k) * per_part, per_part)] = value

        put(0, jnp.where(lower, layer(across), layer(inside)))
        put(1, jnp.where(lower, layer(inside), layer(across)))
        for k, face in enumerate((y_low, y_high, z_low, z_high)):
            value = layer(face)
            put(2 + k, jnp.where(place[1 + k] != 0, value, jnp.zeros_like(value)))

    def pick(k):
        some = pl.ds(pl.multiple_of(k * SOME, SOME), SOME)
        table = lax.broadcasted_iota(jnp.int32, (SOME, ring.shape[0]), 1) == order[some]
        stacked[pl.ds(pl.multiple_of(own_count + k * SOME, SOME), SOME)] = jnp.dot(
            table.astype(jnp.float32).astype(jnp.bfloat16),
            ring[...],
            preferred_element_type=jnp.float32,
        ).astype(jnp.bfloat16)

    pl.loop(0, order.shape[0] // SOME)(pick)

    def ahead(width, i):
        copy(i, width).wait()
        front[rows(i)] = jnp.dot(
            held[rows(i), :width], stacked[:width], preferred_element_type=jnp.float32
        ).astype(jnp.bfloat16)

    def back(skip, j):
        piece = lax.dot_general(
            front[skip:], held[skip:, rows(j)], contract_first, preferred_element_type=jnp.float32
        )
        out[rows(j)] = piece.T

    contract_first = (((0,), (0,)), ((), ()))
    middle = tiles // 2
    pl.loop(0, middle)(functools.partial(ahead, half))
    pl.loop(middle, tiles)(functools.partial(ahead, size))
    pl.loop(0, middle)(functools.partial(back, 0))
    pl.loop(middle, own_count // TILE)(functools.partial(back, half))


def local_solve(place, order, own, faces, factor):
    size, lanes = factor.shape[0], own.shape[-1]
    vmem = pl.BlockSpec(memory_space=pltpu.VMEM)
    return pl.pallas_call(
        local_kernel,
        out_shape=jax.ShapeDtypeStruct(own.shape, jnp.float32),
        in_specs=[pl.BlockSpec(memory_space=pltpu.SMEM)]
        + [vmem] * 8
        + [pl.BlockSpec(memory_space=pltpu.HBM)],
        out_specs=vmem,
        scratch_shapes=[
            pltpu.VMEM((size, size), jnp.bfloat16),
            pltpu.VMEM((size, lanes), jnp.bfloat16),
            pltpu.VMEM((size, lanes), jnp.bfloat16),
            pltpu.VMEM((6 * faces[0].shape[0], lanes), jnp.bfloat16),
            pltpu.SemaphoreType.DMA((size // TILE,)),
        ],
        compiler_params=pltpu.CompilerParams(vmem_limit_bytes=24 * 1024 * 1024),
        name="local_solve",
    )(place, order, own, *faces, factor)


def stack_kernel(place, *refs):
    pieces, (mine, theirs) = refs[:-2], refs[-2:]
    rows, width = pieces[0].shape[0], mine.shape[1]
    for core, out in ((place[1], mine), (1 - place[1], theirs)):
        columns = pl.ds(pl.multiple_of(core * width, width), width)
        for step, piece in enumerate(pieces):
            out[pl.ds(step * rows, rows)] = piece[:, columns]


def stack(coarse_inverse, pieces):
    rows, width = pieces[0].shape
    count = len(pieces) + 1
    place = jnp.stack([lax.axis_index(X), lax.axis_index(C)]).astype(jnp.int32)
    whole = pl.BlockSpec((rows, width), lambda i, place: (0, 0))
    result = pl.BlockSpec((rows * count, width // 2), lambda i, place: (0, 0))
    shape = jax.ShapeDtypeStruct((rows * count, width // 2), coarse_inverse.dtype)
    return pl.pallas_call(
        stack_kernel,
        out_shape=(shape, shape),
        grid_spec=pltpu.PrefetchScalarGridSpec(
            num_scalar_prefetch=1,
            grid=(1,),
            in_specs=[pl.BlockSpec((rows, width), lambda i, place: (0, place[0]))]
            + [whole] * len(pieces),
            out_specs=(result, result),
        ),
        name="stack",
    )(place, coarse_inverse, *pieces)


def spread(coarse_inverse):
    rows, total = coarse_inverse.shape
    count = lax.axis_size(X)
    width = total // count
    at_x = lax.axis_index(X)
    pieces = []
    for step in range(1, count):
        place = (at_x + step) & (count - 1)
        piece = lax.dynamic_slice(coarse_inverse, (0, place * width), (rows, width))
        pieces.append(shift(piece, X, step))
    return stack(coarse_inverse, pieces)


def rolled(value, start, rows):
    doubled = jnp.concatenate([value, value])
    return lax.dynamic_slice(doubled, (start * rows, 0), value.shape)


def gathered(value, blocks):
    rows = value.shape[0]
    at_y, at_z = lax.axis_index(Y), lax.axis_index(Z)
    first, last = ends(blocks, 3)
    z_low = shift(jnp.concatenate([value, last]), Z, 1)
    z_high = shift(jnp.concatenate([value, first]), Z, -1)
    inside, across = swap_faces(blocks)
    pair = jnp.concatenate([z_low[:rows], value])
    three = jnp.concatenate([pair, z_high[:rows]])
    line = jnp.concatenate([shift(three, Z, 3), three, shift(pair, Z, -3)])
    line = rolled(line, (12 - at_z) & 7, rows)
    count = line.shape[0]
    first, last = ends(blocks, 2)
    opposite = shift(line, Y, 2)
    y_low = shift(jnp.concatenate([line, last]), Y, 1)
    y_high = shift(jnp.concatenate([line, first]), Y, 3)
    plane = jnp.concatenate([y_high[:count], opposite, y_low[:count], line])
    return rolled(plane, 3 - at_y, count), (inside, across, y_low, y_high, z_low, z_high)


def coarse_solve(stacks, whole, rows):
    theirs = shift(whole, C, 1)
    parts = jnp.dot(stacks[0], whole, preferred_element_type=jnp.float32)
    parts = parts + jnp.dot(stacks[1], theirs, preferred_element_type=jnp.float32)
    total = parts[:rows]
    for step in range(1, parts.shape[0] // rows):
        part = parts[step * rows : (step + 1) * rows]
        total = total + shift(part, X, -step)
    return total.astype(jnp.bfloat16)


def everywhere(partial):
    for axes in ((*GX, Y[1]), (Y[0], Z)):
        count = 1
        for axis in axes:
            count *= lax.axis_size(axis)
        copies = jnp.broadcast_to(partial[None], (count,) + partial.shape)
        partial = jnp.sum(lax.all_to_all(copies, axes, 0, 0, tiled=True), axis=0)
    return partial


def local(right_side, stiffness, local_factor, basis, coarse_map, margin_index, coarse_inverse):
    factor = local_factor.reshape(local_factor.shape[-2:])
    basis_count = basis.shape[-2]
    coarse_ids = coarse_map.reshape(-1)
    order = margin_index.reshape(-1, 1)
    placement = (
        coarse_ids[None, :] == lax.broadcasted_iota(jnp.int32, (basis_count, basis_count), 0)
    ).astype(jnp.bfloat16)
    functions = jnp.dot(
        placement, basis.reshape(basis.shape[-2:]), preferred_element_type=jnp.float32
    ).astype(jnp.bfloat16)
    contract_first = (((0,), (0,)), ((), ()))
    at_y, at_z = lax.axis_index(Y), lax.axis_index(Z)
    place = jnp.stack(
        [
            lax.axis_index(C),
            at_y > 0,
            at_y < lax.axis_size(Y) - 1,
            at_z > 0,
            at_z < lax.axis_size(Z) - 1,
        ]
    ).astype(jnp.int32)
    diagonal = 6.0 + stiffness[..., None]
    stacks = spread(coarse_inverse)

    def precondition(field):
        rounded = field.astype(jnp.bfloat16)
        own_rows = rounded.reshape(-1, rounded.shape[-1])
        placed = jnp.dot(functions, own_rows, preferred_element_type=jnp.float32).astype(
            jnp.bfloat16
        )
        whole, faces = gathered(placed, rounded)
        local_part = local_solve(place, order, own_rows, faces, factor)
        solved = coarse_solve(stacks, whole, basis_count)
        coarse_part = lax.dot_general(
            functions, solved, contract_first, preferred_element_type=jnp.float32
        )
        return (local_part + coarse_part).reshape(field.shape)

    def operate(field):
        faces = halo(field.astype(jnp.bfloat16))
        beside = None
        for dim in (1, 2, 3):
            shape = list(field.shape)
            shape[dim] = 1
            low, high = (
                face.astype(field.dtype).reshape(shape) for face in faces[2 * dim - 2 : 2 * dim]
            )
            length = field.shape[dim]
            before = jnp.concatenate([low, lax.slice_in_dim(field, 0, length - 1, axis=dim)], dim)
            after = jnp.concatenate([lax.slice_in_dim(field, 1, length, axis=dim), high], dim)
            beside = before + after if beside is None else beside + before + after
        return diagonal * field - beside

    raw = right_side * SCALE
    search_one = precondition(raw)
    image_one = operate(search_one)
    search_two = precondition(image_one)
    image_two = operate(search_two)
    gram = everywhere(
        jnp.stack(
            [
                inner(raw, raw),
                inner(image_one, raw),
                inner(image_one, image_one),
                inner(image_two, raw),
                inner(image_two, image_one),
                inner(image_two, image_two),
            ]
        )
    )
    weight_one, weight_two, ratio = weights(gram)
    return (weight_one * search_one + weight_two * search_two, ratio)


def solution(mesh):
    finer = Mesh(
        mesh.devices.reshape(4, 2, 2, 2, mesh.shape["gz"]), ("gx_0", "gx_1", "gy_0", "gy_1", "gz")
    )
    placed = (
        P(None, GX, Y, Z, None),
        P(None, GX, Y, Z),
        P(GX, Y, Z, None, None),
        P(GX, Y, Z, None, None),
        P(GX, Y, Z, None),
        P(GX, Y, Z, None),
        P(GX_GY_GZ, None),
    )
    return jax.shard_map(
        local,
        mesh=finer,
        in_specs=placed,
        out_specs=(P(None, GX, Y, Z, None), P()),
        check_vma=False,
    )
```

profile of v0, /device:TPU:8, one launch (start us, length us, event | category | flops | bytes accessed | tf_op | source)
XLA Modules:
  0.0 197.8 jit_solution(12290346366066752096)
XLA Ops:
  0.7 1.4 fusion.8
  2.7 0.6 pad_maximum_fusion.5
  3.4 1.9 collective-permute-start.2
  5.3 3.9 %collective-permute-start.3 = (bf16[256,128]{1,0:T(8,128)(2,1)}, bf16[256,128]{1,0:T(8,128)(2,1)S(1)}, u32[]{:S(2)}, u32[]{:S(2)}) collective-permute-start(bf16[256,128]{1,0:T(8,128)(2,1)} %get-tuple-element.83), channel_id=1, source_target_pairs={{0,7},{1,0},{2,1},{3,2},{4,3},{5,4},{6,5},{7,6},{8,15},{9,8},{10,9... | collective-permute-start | bytes 196616 | tf_op jit(solution)/shard_map/ppermute | solution.py:24
  9.3 0.8 fusion.54
  10.0 1.5 copy.140
  11.5 0.6 copy.139
  12.2 4.7 %collective-permute-start.4 = (bf16[192,128]{1,0:T(8,128)(2,1)S(1)}, bf16[192,128]{1,0:T(8,128)(2,1)S(1)}, u32[]{:S(2)}, u32[]{:S(2)}) collective-permute-start(bf16[192,128]{1,0:T(8,128)(2,1)S(1)} %pad_maximum_fusion.8), channel_id=1, source_target_pairs={{0,3},{1,4},{2,5},{3,6},{4,7},{5,0},{6,1},{7,2},{8,11},{9,12},{10,... | collective-permute-start | bytes 147464 | tf_op jit(solution)/shard_map/ppermute | solution.py:24
  17.3 2.6 %collective-permute-done.4 = bf16[192,128]{1,0:T(8,128)(2,1)S(1)} collective-permute-done((bf16[192,128]{1,0:T(8,128)(2,1)S(1)}, bf16[192,128]{1,0:T(8,128)(2,1)S(1)}, u32[]{:S(2)}, u32[]{:S(2)}) %collective-permute-start.4) | collective-permute-done | bytes 49184 | tf_op jit(solution)/shard_map/ppermute | solution.py:24
  26.3 1.6 constant_dynamic-slice_fusion.6
  27.8 1.7 pad_maximum_fusion
  30.0 1.2 constant_dynamic-slice_fusion.3
  31.2 2.8 %collective-permute-start.10 = (bf16[64,4096]{1,0:T(8,128)(2,1)}, bf16[64,4096]{1,0:T(8,128)(2,1)S(1)}, u32[]{:S(2)}, u32[]{:S(2)}) collective-permute-start(bf16[64,4096]{1,0:T(8,128)(2,1)} %get-tuple-element.27), channel_id=1, source_target_pairs={{0,192},{64,0},{128,64},{192,128},{1,193},{65,1},{129,65},{193,129... | collective-permute-start | bytes 1572872 | tf_op jit(solution)/shard_map/ppermute | solution.py:24
  33.9 0.8 collective-permute-start.9
  34.7 0.9 collective-permute-start.8
  35.6 2.6 %collective-permute-start.11 = (bf16[512,128]{1,0:T(8,128)(2,1)}, bf16[512,128]{1,0:T(8,128)(2,1)S(1)}, u32[]{:S(2)}, u32[]{:S(2)}) collective-permute-start(bf16[512,128]{1,0:T(8,128)(2,1)} %constant_dynamic-slice_fusion.6), channel_id=1, source_target_pairs={{0,16},{8,24},{16,0},{24,8},{1,17},{9,25},{17,1},{25,9},{2,18},{10... | collective-permute-start | bytes 393224 | tf_op jit(solution)/shard_map/ppermute | solution.py:24
  38.2 1.9 collective-permute-start.6
  40.1 2.2 %collective-permute-done.11 = bf16[512,128]{1,0:T(8,128)(2,1)S(1)} collective-permute-done((bf16[512,128]{1,0:T(8,128)(2,1)}, bf16[512,128]{1,0:T(8,128)(2,1)S(1)}, u32[]{:S(2)}, u32[]{:S(2)}) %collective-permute-start.11) | collective-permute-done | bytes 131104 | tf_op jit(solution)/shard_map/ppermute | solution.py:24
  42.3 2.0 %collective-permute-done.6.rest_2_ = bf16[704,128]{1,0:T(8,128)(2,1)S(1)} collective-permute-done((bf16[704,128]{1,0:T(8,128)(2,1)}, bf16[704,128]{1,0:T(8,128)(2,1)S(1)}, u32[]{:S(2)}, u32[]{:S(2)}) %collective-permute-start.6) | collective-permute-done | bytes 180256 | tf_op jit(solution)/shard_map/ppermute | solution.py:24
  44.4 0.9 constant_dynamic-update-slice_fusion.12
  45.4 0.9 constant_dynamic-update-slice_fusion.10
  46.5 0.8 broadcast_select_fusion.10
  49.6 5.1 %collective-permute-done.10.refs_3_ = bf16[64,4096]{1,0:T(8,128)(2,1)S(1)} collective-permute-done((bf16[64,4096]{1,0:T(8,128)(2,1)}, bf16[64,4096]{1,0:T(8,128)(2,1)S(1)}, u32[]{:S(2)}, u32[]{:S(2)}) %collective-permute-start.10) | collective-permute-done | bytes 524320 | tf_op jit(solution)/shard_map/ppermute | solution.py:24
  54.7 0.7 collective-permute-start.1
  55.4 3.0 %collective-permute-done.8.refs_1_ = bf16[64,4096]{1,0:T(8,128)(2,1)} collective-permute-done((bf16[64,4096]{1,0:T(8,128)(2,1)}, bf16[64,4096]{1,0:T(8,128)(2,1)}, u32[]{:S(2)}, u32[]{:S(2)}) %collective-permute-start.8) | collective-permute-done | bytes 524320 | tf_op jit(solution)/shard_map/ppermute | solution.py:24
  58.4 3.7 %stack.82 = (bf16[256,2048]{1,0:T(8,128)(2,1)}, bf16[256,2048]{1,0:T(8,128)(2,1)}) custom-call(s32[2]{0:T(128)} %pad_add_fusion.place, bf16[64,16384]{1,0:T(8,128)(2,1)} %refs_0_.1, bf16[64,4096]{1,0:T(8,128)(2,1)} %collective-permute-done.8.refs_1_, bf16[64,4096]{1,0:T(8,128)(2,1)} %copy-done.10, bf16[64,4096]{1,0:T(8,128)(2,1)} %copy-done.9), custom_call_target="tpu_custom_call" | custom-call | tf_op jit(solution)/shard_map/stack/pallas_call | solution.py:209
  62.1 1.7 fusion.58
  63.7 1.6 convolution_add_fusion.1
  65.4 2.7 %collective-permute-start.13 = (f32[64,128]{1,0:T(8,128)S(1)}, f32[64,128]{1,0:T(8,128)S(1)}, u32[]{:S(2)}, u32[]{:S(2)}) collective-permute-start(f32[64,128]{1,0:T(8,128)S(1)} %get-tuple-element.71), channel_id=1, source_target_pairs={{0,192},{64,0},{128,64},{192,128},{1,193},{65,1},{129,65},{193,129... | collective-permute-start | bytes 98312 | tf_op jit(solution)/shard_map/ppermute | solution.py:24
  68.1 1.7 collective-permute-start.14
  70.3 3.4 %copy-done.1 = bf16[1,1,1,2048,2048]{4,3,2,1,0:T(8,128)(2,1)S(1)} copy-done((bf16[1,1,1,2048,2048]{4,3,2,1,0:T(8,128)(2,1)S(1)}, bf16[1,1,1,2048,2048]{4,3,2,1,0:T(8,128)(2,1)}, u32[]{:S(2)}) %copy-start.1) | copy-done | bytes 8388632
  73.7 7.7 %local_solve.2 = f32[1536,128]{1,0:T(8,128)S(1)} custom-call(s32[5]{0:T(128)S(1)} %stack.69.place, s32[512,1]{1,0:T(8,128)S(1)} %copy.141.order, bf16[1536,128]{1,0:T(8,128)(2,1)S(1)} %bitcast.197, bf16[192,128]{1,0:T(8,128)(2,1)S(1)} %collective-permute-done.rest_0_, bf16[192,128]{1,0:T(8,128)(2,1)S(1)} %collective-permute-done.1.rest_1_, ...), custom_call_target="tpu_custom_call" | custom-call | tf_op jit(solution)/shard_map/local_solve/pallas_call | solution.py:174
  82.6 1.1 collective-permute-start.17
  83.7 0.7 collective-permute-start.16
  84.5 4.9 %collective-permute-start.19 = (bf16[192,128]{1,0:T(8,128)(2,1)S(1)}, bf16[192,128]{1,0:T(8,128)(2,1)S(1)}, u32[]{:S(2)}, u32[]{:S(2)}) collective-permute-start(bf16[192,128]{1,0:T(8,128)(2,1)S(1)} %bitcast.241), channel_id=1, source_target_pairs={{8,0},{16,8},{24,16},{9,1},{17,9},{25,17},{10,2},{18,10},{26,18},{... | collective-permute-start | bytes 147464 | tf_op jit(solution)/shard_map/ppermute | solution.py:54
  89.4 1.3 collective-permute-start.21
  90.7 4.5 %collective-permute-start.20 = (bf16[192,128]{1,0:T(8,128)(2,1)S(1)}, bf16[192,128]{1,0:T(8,128)(2,1)S(1)}, u32[]{:S(2)}, u32[]{:S(2)}) collective-permute-start(bf16[192,128]{1,0:T(8,128)(2,1)S(1)} %bitcast.232), channel_id=1, source_target_pairs={{0,1},{1,2},{2,3},{3,4},{4,5},{5,6},{6,7},{8,9},{9,10},{10,11},{11... | collective-permute-start | bytes 147464 | tf_op jit(solution)/shard_map/ppermute | solution.py:53
  96.1 1.9 collective-permute-start.18
  98.3 3.8 %collective-permute-done.18 = bf16[192,128]{1,0:T(8,128)(2,1)S(1)} collective-permute-done((bf16[192,128]{1,0:T(8,128)(2,1)S(1)}, bf16[192,128]{1,0:T(8,128)(2,1)S(1)}, u32[]{:S(2)}, u32[]{:S(2)}) %collective-permute-start.18) | collective-permute-done | bytes 49184 | tf_op jit(solution)/shard_map/ppermute | solution.py:53
  102.2 0.7 fusion.9
  103.9 1.6 collective-permute-start.24
  105.5 1.7 collective-permute-start.25
  107.4 2.5 %collective-permute-done.24.rest_4_ = bf16[256,128]{1,0:T(8,128)(2,1)S(1)} collective-permute-done((bf16[256,128]{1,0:T(8,128)(2,1)S(1)}, bf16[256,128]{1,0:T(8,128)(2,1)S(1)}, u32[]{:S(2)}, u32[]{:S(2)}) %collective-permute-start.24) | collective-permute-done | bytes 65568 | tf_op jit(solution)/shard_map/ppermute | solution.py:24
  110.0 4.7 %collective-permute-start.26 = (bf16[192,128]{1,0:T(8,128)(2,1)S(1)}, bf16[192,128]{1,0:T(8,128)(2,1)S(1)}, u32[]{:S(2)}, u32[]{:S(2)}) collective-permute-start(bf16[192,128]{1,0:T(8,128)(2,1)S(1)} %pad_maximum_fusion.9), channel_id=1, source_target_pairs={{0,3},{1,4},{2,5},{3,6},{4,7},{5,0},{6,1},{7,2},{8,11},{9,12},{10,... | collective-permute-start | bytes 147464 | tf_op jit(solution)/shard_map/ppermute | solution.py:24
  115.1 2.4 %collective-permute-done.26 = bf16[192,128]{1,0:T(8,128)(2,1)S(1)} collective-permute-done((bf16[192,128]{1,0:T(8,128)(2,1)S(1)}, bf16[192,128]{1,0:T(8,128)(2,1)S(1)}, u32[]{:S(2)}, u32[]{:S(2)}) %collective-permute-start.26) | collective-permute-done | bytes 49184 | tf_op jit(solution)/shard_map/ppermute | solution.py:24
  117.5 3.4 %collective-permute-done.27 = bf16[128,128]{1,0:T(8,128)(2,1)S(1)} collective-permute-done((bf16[128,128]{1,0:T(8,128)(2,1)S(1)}, bf16[128,128]{1,0:T(8,128)(2,1)S(1)}, u32[]{:S(2)}, u32[]{:S(2)}) %collective-permute-start.27) | collective-permute-done | bytes 32800 | tf_op jit(solution)/shard_map/ppermute | solution.py:24
  121.2 1.3 collective-permute-start.30
  122.5 1.4 collective-permute-start.28
  123.9 4.6 %collective-permute-done.29.rest_3_ = bf16[704,128]{1,0:T(8,128)(2,1)S(1)} collective-permute-done((bf16[704,128]{1,0:T(8,128)(2,1)S(1)}, bf16[704,128]{1,0:T(8,128)(2,1)S(1)}, u32[]{:S(2)}, u32[]{:S(2)}) %collective-permute-start.29) | collective-permute-done | bytes 180256 | tf_op jit(solution)/shard_map/ppermute | solution.py:24
  128.5 1.8 collective-permute-done.28.rest_2_
  131.3 0.7 collective-permute-start.23
  133.4 4.9 %collective-permute-start.32 = (f32[64,128]{1,0:T(8,128)S(1)}, f32[64,128]{1,0:T(8,128)S(1)}, u32[]{:S(2)}, u32[]{:S(2)}) collective-permute-start(f32[64,128]{1,0:T(8,128)S(1)} %get-tuple-element.66), channel_id=1, source_target_pairs={{0,192},{64,0},{128,64},{192,128},{1,193},{65,1},{129,65},{193,129... | collective-permute-start | bytes 98312 | tf_op jit(solution)/shard_map/ppermute | solution.py:24
  138.3 1.8 collective-permute-start.33
  140.2 7.7 %local_solve.3 = f32[1536,128]{1,0:T(8,128)S(1)} custom-call(s32[5]{0:T(128)S(1)} %stack.69.place, s32[512,1]{1,0:T(8,128)S(1)} %copy.141.order, bf16[1536,128]{1,0:T(8,128)(2,1)S(1)} %get-tuple-element.25.own, bf16[192,128]{1,0:T(8,128)(2,1)S(1)} %collective-permute-done.22.rest_0_, bf16[192,128]{1,0:T(8,128)(2,1)S(1)} %collective-permute-done.23.rest_1_, ...), custom_call_target="tpu_custom_call" | custom-call | tf_op jit(solution)/shard_map/local_solve/pallas_call | solution.py:174
  149.2 0.7 collective-permute-start.35
  150.0 3.7 %collective-permute-start.38 = (bf16[192,128]{1,0:T(8,128)(2,1)S(1)}, bf16[192,128]{1,0:T(8,128)(2,1)S(1)}, u32[]{:S(2)}, u32[]{:S(2)}) collective-permute-start(bf16[192,128]{1,0:T(8,128)(2,1)S(1)} %bitcast.239), channel_id=1, source_target_pairs={{8,0},{16,8},{24,16},{9,1},{17,9},{25,17},{10,2},{18,10},{26,18},{... | collective-permute-start | bytes 147464 | tf_op jit(solution)/shard_map/ppermute | solution.py:54
  153.7 1.3 collective-permute-start.40
  155.0 4.6 %collective-permute-start.39 = (bf16[192,128]{1,0:T(8,128)(2,1)S(1)}, bf16[192,128]{1,0:T(8,128)(2,1)S(1)}, u32[]{:S(2)}, u32[]{:S(2)}) collective-permute-start(bf16[192,128]{1,0:T(8,128)(2,1)S(1)} %bitcast.231), channel_id=1, source_target_pairs={{0,1},{1,2},{2,3},{3,4},{4,5},{5,6},{6,7},{8,9},{9,10},{10,11},{11... | collective-permute-start | bytes 147464 | tf_op jit(solution)/shard_map/ppermute | solution.py:53
  160.5 2.1 %collective-permute-start.37 = (bf16[192,128]{1,0:T(8,128)(2,1)S(1)}, bf16[192,128]{1,0:T(8,128)(2,1)S(1)}, u32[]{:S(2)}, u32[]{:S(2)}) collective-permute-start(bf16[192,128]{1,0:T(8,128)(2,1)S(1)} %bitcast.229), channel_id=1, source_target_pairs={{0,8},{8,16},{16,24},{1,9},{9,17},{17,25},{2,10},{10,18},{18,26},{... | collective-permute-start | bytes 147464 | tf_op jit(solution)/shard_map/ppermute | solution.py:53
  162.9 3.6 %collective-permute-done.37 = bf16[192,128]{1,0:T(8,128)(2,1)S(1)} collective-permute-done((bf16[192,128]{1,0:T(8,128)(2,1)S(1)}, bf16[192,128]{1,0:T(8,128)(2,1)S(1)}, u32[]{:S(2)}, u32[]{:S(2)}) %collective-permute-start.37) | collective-permute-done | bytes 49184 | tf_op jit(solution)/shard_map/ppermute | solution.py:53
  166.6 1.4 multiply_reduce_fusion.2
  168.8 13.2 %all_to_all.10 = f32[16,6,128]{2,1,0:T(8,128)S(1)} all-to-all(f32[16,6,128]{2,1,0:T(8,128)S(1)} %broadcast_in_dim.4), channel_id=1, replica_groups=mesh['gx_0'=4,'gx_1'=2,'gy_0'=2,'gy_1'=2,'gz'=8] {'gx_0','gx_1','gy_1'}, dimensions={0} | all-to-all | bytes 98304 | tf_op jit(solution)/shard_map/all_to_all | solution.py:278
  182.0 14.0 %all_to_all.11 = f32[16,6,128]{2,1,0:T(8,128)S(1)} all-to-all(f32[16,6,128]{2,1,0:T(8,128)S(1)} %broadcast_in_dim.5), channel_id=1, replica_groups=mesh['gx_0'=4,'gx_1'=2,'gy_0'=2,'gy_1'=2,'gz'=8] {'gy_0','gz'}, dimensions={0} | all-to-all | bytes 98304 | tf_op jit(solution)/shard_map/all_to_all | solution.py:278
  196.7 1.0 multiply_add_fusion
  (206 shorter events, 21.2 us)
Async XLA Ops:
  0.6 1.7 copy-start
  0.6 1.7 copy-start.13
  2.0 27.5 %copy-start.7 = (bf16[3,8,8,8,128]{4,2,1,0,3:T(8,128)(2,1)}, bf16[3,8,8,8,128]{4,2,1,0,3:T(8,128)(2,1)S(1)}, u32[]{:S(2)}) copy-start(bf16[3,8,8,8,128]{4,2,1,0,3:T(8,128)(2,1)S(1)} %fusion.8) | copy-start | bytes 1179652
  2.0 28.0 %copy-start.2 = (bf16[64,16384]{1,0:T(8,128)(2,1)S(1)}, bf16[64,16384]{1,0:T(8,128)(2,1)}, u32[]{:S(2)}) copy-start(bf16[64,16384]{1,0:T(8,128)(2,1)} %refs_0_.1) | copy-start | bytes 6291460
  2.5 28.6 %copy-start.3 = (bf16[64,1536]{1,0:T(8,128)(2,1)}, bf16[64,1536]{1,0:T(8,128)(2,1)S(1)}, u32[]{:S(2)}) copy-start(bf16[64,1536]{1,0:T(8,128)(2,1)S(1)} %convolution_convert_fusion) | copy-start | bytes 589828
  3.4 8.8 %collective-permute-start.2 = (bf16[256,128]{1,0:T(8,128)(2,1)}, bf16[256,128]{1,0:T(8,128)(2,1)S(1)}, u32[]{:S(2)}, u32[]{:S(2)}) collective-permute-start(bf16[256,128]{1,0:T(8,128)(2,1)} %get-tuple-element.82), channel_id=1, source_target_pairs={{0,1},{1,2},{2,3},{3,4},{4,5},{5,6},{6,7},{7,0},{8,9},{9,10},{10,1... | collective-permute-start | bytes 196616 | tf_op jit(solution)/shard_map/ppermute | solution.py:24
  5.3 6.9 %collective-permute-start.3 = (bf16[256,128]{1,0:T(8,128)(2,1)}, bf16[256,128]{1,0:T(8,128)(2,1)S(1)}, u32[]{:S(2)}, u32[]{:S(2)}) collective-permute-start(bf16[256,128]{1,0:T(8,128)(2,1)} %get-tuple-element.83), channel_id=1, source_target_pairs={{0,7},{1,0},{2,1},{3,2},{4,3},{5,4},{6,5},{7,6},{8,15},{9,8},{10,9... | collective-permute-start | bytes 196616 | tf_op jit(solution)/shard_map/ppermute | solution.py:24
  12.2 7.7 %collective-permute-start.4 = (bf16[192,128]{1,0:T(8,128)(2,1)S(1)}, bf16[192,128]{1,0:T(8,128)(2,1)S(1)}, u32[]{:S(2)}, u32[]{:S(2)}) collective-permute-start(bf16[192,128]{1,0:T(8,128)(2,1)S(1)} %pad_maximum_fusion.8), channel_id=1, source_target_pairs={{0,3},{1,4},{2,5},{3,6},{4,7},{5,0},{6,1},{7,2},{8,11},{9,12},{10,... | collective-permute-start | bytes 147464 | tf_op jit(solution)/shard_map/ppermute | solution.py:24
  16.9 5.7 %collective-permute-start.5 = (bf16[128,128]{1,0:T(8,128)(2,1)S(1)}, bf16[128,128]{1,0:T(8,128)(2,1)S(1)}, u32[]{:S(2)}, u32[]{:S(2)}) collective-permute-start(bf16[128,128]{1,0:T(8,128)(2,1)S(1)} %pad_maximum_fusion.10), channel_id=1, source_target_pairs={{0,5},{1,6},{2,7},{3,0},{4,1},{5,2},{6,3},{7,4},{8,13},{9,14},{10,... | collective-permute-start | bytes 98312 | tf_op jit(solution)/shard_map/ppermute | solution.py:24
  29.5 8.7 %collective-permute-start.7 = (bf16[704,128]{1,0:T(8,128)(2,1)}, bf16[704,128]{1,0:T(8,128)(2,1)S(1)}, u32[]{:S(2)}, u32[]{:S(2)}) collective-permute-start(bf16[704,128]{1,0:T(8,128)(2,1)} %get-tuple-element.74), channel_id=1, source_target_pairs={{0,24},{8,0},{16,8},{24,16},{1,25},{9,1},{17,9},{25,17},{2,26},{10... | collective-permute-start | bytes 540680 | tf_op jit(solution)/shard_map/ppermute | solution.py:24
  31.2 23.5 %collective-permute-start.10 = (bf16[64,4096]{1,0:T(8,128)(2,1)}, bf16[64,4096]{1,0:T(8,128)(2,1)S(1)}, u32[]{:S(2)}, u32[]{:S(2)}) collective-permute-start(bf16[64,4096]{1,0:T(8,128)(2,1)} %get-tuple-element.27), channel_id=1, source_target_pairs={{0,192},{64,0},{128,64},{192,128},{1,193},{65,1},{129,65},{193,129... | collective-permute-start | bytes 1572872 | tf_op jit(solution)/shard_map/ppermute | solution.py:24
  33.9 21.4 %collective-permute-start.9 = (bf16[64,4096]{1,0:T(8,128)(2,1)}, bf16[64,4096]{1,0:T(8,128)(2,1)S(1)}, u32[]{:S(2)}, u32[]{:S(2)}) collective-permute-start(bf16[64,4096]{1,0:T(8,128)(2,1)} %get-tuple-element.28), channel_id=1, source_target_pairs={{0,128},{64,192},{128,0},{192,64},{1,129},{65,193},{129,1},{193,65... | collective-permute-start | bytes 1572872 | tf_op jit(solution)/shard_map/ppermute | solution.py:24
  34.7 23.7 %collective-permute-start.8 = (bf16[64,4096]{1,0:T(8,128)(2,1)}, bf16[64,4096]{1,0:T(8,128)(2,1)}, u32[]{:S(2)}, u32[]{:S(2)}) collective-permute-start(bf16[64,4096]{1,0:T(8,128)(2,1)} %get-tuple-element.29), channel_id=1, source_target_pairs={{0,64},{64,128},{128,192},{192,0},{1,65},{65,129},{129,193},{193,1... | collective-permute-start | bytes 1572872 | tf_op jit(solution)/shard_map/ppermute | solution.py:24
  35.6 6.7 %collective-permute-start.11 = (bf16[512,128]{1,0:T(8,128)(2,1)}, bf16[512,128]{1,0:T(8,128)(2,1)S(1)}, u32[]{:S(2)}, u32[]{:S(2)}) collective-permute-start(bf16[512,128]{1,0:T(8,128)(2,1)} %constant_dynamic-slice_fusion.6), channel_id=1, source_target_pairs={{0,16},{8,24},{16,0},{24,8},{1,17},{9,25},{17,1},{25,9},{2,18},{10... | collective-permute-start | bytes 393224 | tf_op jit(solution)/shard_map/ppermute | solution.py:24
  38.2 6.1 %collective-permute-start.6 = (bf16[704,128]{1,0:T(8,128)(2,1)}, bf16[704,128]{1,0:T(8,128)(2,1)S(1)}, u32[]{:S(2)}, u32[]{:S(2)}) collective-permute-start(bf16[704,128]{1,0:T(8,128)(2,1)} %get-tuple-element.75), channel_id=1, source_target_pairs={{0,8},{8,16},{16,24},{24,0},{1,9},{9,17},{17,25},{25,1},{2,10},{10... | collective-permute-start | bytes 540680 | tf_op jit(solution)/shard_map/ppermute | solution.py:24
  46.4 15.7 %collective-permute-start.12 = (bf16[2048,128]{1,0:T(8,128)(2,1)S(1)}, bf16[2048,128]{1,0:T(8,128)(2,1)S(1)}, u32[]{:S(2)}, u32[]{:S(2)}) collective-permute-start(bf16[2048,128]{1,0:T(8,128)(2,1)S(1)} %constant_dynamic-slice_fusion.2), channel_id=1, source_target_pairs={{0,32},{32,0},{1,33},{33,1},{2,34},{34,2},{3,35},{35,3},{4,36},{36... | collective-permute-start | bytes 1572872 | tf_op jit(solution)/shard_map/ppermute | solution.py:24
  47.9 22.4 %collective-permute-start = (bf16[192,128]{1,0:T(8,128)(2,1)}, bf16[192,128]{1,0:T(8,128)(2,1)S(1)}, u32[]{:S(2)}, u32[]{:S(2)}) collective-permute-start(bf16[192,128]{1,0:T(8,128)(2,1)} %bitcast.8), channel_id=1, source_target_pairs={{0,32},{32,0},{1,33},{33,1},{2,34},{34,2},{3,35},{35,3},{4,36},{36... | collective-permute-start | bytes 147464 | tf_op jit(solution)/shard_map/ppermute | solution.py:24
  54.7 3.7 %copy-start.9 = (bf16[64,4096]{1,0:T(8,128)(2,1)}, bf16[64,4096]{1,0:T(8,128)(2,1)S(1)}, u32[]{:S(2)}) copy-start(bf16[64,4096]{1,0:T(8,128)(2,1)S(1)} %collective-permute-done.10.refs_3_) | copy-start | bytes 1572868
  54.7 15.6 %collective-permute-start.1 = (bf16[192,128]{1,0:T(8,128)(2,1)}, bf16[192,128]{1,0:T(8,128)(2,1)S(1)}, u32[]{:S(2)}, u32[]{:S(2)}) collective-permute-start(bf16[192,128]{1,0:T(8,128)(2,1)} %bitcast.9), channel_id=1, source_target_pairs={{32,64},{96,128},{160,192},{64,32},{128,96},{192,160},{33,65},{97,... | collective-permute-start | bytes 147464 | tf_op jit(solution)/shard_map/ppermute | solution.py:40
  55.4 3.0 %copy-start.10 = (bf16[64,4096]{1,0:T(8,128)(2,1)}, bf16[64,4096]{1,0:T(8,128)(2,1)S(1)}, u32[]{:S(2)}) copy-start(bf16[64,4096]{1,0:T(8,128)(2,1)S(1)} %collective-permute-done.9.refs_2_) | copy-start | bytes 1572868
  62.0 7.8 %copy-start.11 = (f32[3,8,8,8]{3,2,1,0:T(8,128)S(1)}, f32[3,8,8,8]{3,2,1,0:T(8,128)}, u32[]{:S(2)}) copy-start(f32[3,8,8,8]{3,2,1,0:T(8,128)} %param.8) | copy-start | bytes 18436
  62.1 8.0 %copy-start.12 = (s32[1,1,1,512]{3,2,1,0:T(1,128)S(1)}, s32[1,1,1,512]{3,2,1,0:T(1,128)}, u32[]{:S(2)}) copy-start(s32[1,1,1,512]{3,2,1,0:T(1,128)} %param.12) | copy-start | bytes 6148
  65.4 16.0 %collective-permute-start.13 = (f32[64,128]{1,0:T(8,128)S(1)}, f32[64,128]{1,0:T(8,128)S(1)}, u32[]{:S(2)}, u32[]{:S(2)}) collective-permute-start(f32[64,128]{1,0:T(8,128)S(1)} %get-tuple-element.71), channel_id=1, source_target_pairs={{0,192},{64,0},{128,64},{192,128},{1,193},{65,1},{129,65},{193,129... | collective-permute-start | bytes 98312 | tf_op jit(solution)/shard_map/ppermute | solution.py:24
  68.1 13.3 %collective-permute-start.15 = (f32[64,128]{1,0:T(8,128)S(1)}, f32[64,128]{1,0:T(8,128)S(1)}, u32[]{:S(2)}, u32[]{:S(2)}) collective-permute-start(f32[64,128]{1,0:T(8,128)S(1)} %get-tuple-element.72), channel_id=1, source_target_pairs={{0,64},{64,128},{128,192},{192,0},{1,65},{65,129},{129,193},{193,1... | collective-permute-start | bytes 98312 | tf_op jit(solution)/shard_map/ppermute | solution.py:24
  68.1 13.3 %collective-permute-start.14 = (f32[64,128]{1,0:T(8,128)S(1)}, f32[64,128]{1,0:T(8,128)S(1)}, u32[]{:S(2)}, u32[]{:S(2)}) collective-permute-start(f32[64,128]{1,0:T(8,128)S(1)} %get-tuple-element.73), channel_id=1, source_target_pairs={{0,128},{64,192},{128,0},{192,64},{1,129},{65,193},{129,1},{193,65... | collective-permute-start | bytes 98312 | tf_op jit(solution)/shard_map/ppermute | solution.py:24
  70.3 3.4 %copy-start.1 = (bf16[1,1,1,2048,2048]{4,3,2,1,0:T(8,128)(2,1)S(1)}, bf16[1,1,1,2048,2048]{4,3,2,1,0:T(8,128)(2,1)}, u32[]{:S(2)}) copy-start(bf16[1,1,1,2048,2048]{4,3,2,1,0:T(8,128)(2,1)} %param.9) | copy-start | bytes 25165828
  73.7 7.7 %copy-start.4 = (bf16[64,1536]{1,0:T(8,128)(2,1)S(1)}, bf16[64,1536]{1,0:T(8,128)(2,1)}, u32[]{:S(2)}) copy-start(bf16[64,1536]{1,0:T(8,128)(2,1)} %copy-done.3) | copy-start | bytes 589828
  82.6 13.5 %collective-permute-start.17 = (bf16[192,128]{1,0:T(8,128)(2,1)S(1)}, bf16[192,128]{1,0:T(8,128)(2,1)S(1)}, u32[]{:S(2)}, u32[]{:S(2)}) collective-permute-start(bf16[192,128]{1,0:T(8,128)(2,1)S(1)} %bitcast.225), channel_id=1, source_target_pairs={{0,32},{32,0},{1,33},{33,1},{2,34},{34,2},{3,35},{35,3},{4,36},{36... | collective-permute-start | bytes 147464 | tf_op jit(solution)/shard_map/ppermute | solution.py:24
  83.7 14.4 %collective-permute-start.16 = (bf16[192,128]{1,0:T(8,128)(2,1)S(1)}, bf16[192,128]{1,0:T(8,128)(2,1)S(1)}, u32[]{:S(2)}, u32[]{:S(2)}) collective-permute-start(bf16[192,128]{1,0:T(8,128)(2,1)S(1)} %bitcast.223), channel_id=1, source_target_pairs={{32,64},{96,128},{160,192},{64,32},{128,96},{192,160},{33,65},{97,... | collective-permute-start | bytes 147464 | tf_op jit(solution)/shard_map/ppermute | solution.py:40
  84.5 13.7 %collective-permute-start.19 = (bf16[192,128]{1,0:T(8,128)(2,1)S(1)}, bf16[192,128]{1,0:T(8,128)(2,1)S(1)}, u32[]{:S(2)}, u32[]{:S(2)}) collective-permute-start(bf16[192,128]{1,0:T(8,128)(2,1)S(1)} %bitcast.241), channel_id=1, source_target_pairs={{8,0},{16,8},{24,16},{9,1},{17,9},{25,17},{10,2},{18,10},{26,18},{... | collective-permute-start | bytes 147464 | tf_op jit(solution)/shard_map/ppermute | solution.py:54
  89.4 8.9 %collective-permute-start.21 = (bf16[192,128]{1,0:T(8,128)(2,1)S(1)}, bf16[192,128]{1,0:T(8,128)(2,1)S(1)}, u32[]{:S(2)}, u32[]{:S(2)}) collective-permute-start(bf16[192,128]{1,0:T(8,128)(2,1)S(1)} %bitcast.234), channel_id=1, source_target_pairs={{1,0},{2,1},{3,2},{4,3},{5,4},{6,5},{7,6},{9,8},{10,9},{11,10},{12... | collective-permute-start | bytes 147464 | tf_op jit(solution)/shard_map/ppermute | solution.py:54
  90.7 7.6 %collective-permute-start.20 = (bf16[192,128]{1,0:T(8,128)(2,1)S(1)}, bf16[192,128]{1,0:T(8,128)(2,1)S(1)}, u32[]{:S(2)}, u32[]{:S(2)}) collective-permute-start(bf16[192,128]{1,0:T(8,128)(2,1)S(1)} %bitcast.232), channel_id=1, source_target_pairs={{0,1},{1,2},{2,3},{3,4},{4,5},{5,6},{6,7},{8,9},{9,10},{10,11},{11... | collective-permute-start | bytes 147464 | tf_op jit(solution)/shard_map/ppermute | solution.py:53
  96.1 6.0 %collective-permute-start.18 = (bf16[192,128]{1,0:T(8,128)(2,1)S(1)}, bf16[192,128]{1,0:T(8,128)(2,1)S(1)}, u32[]{:S(2)}, u32[]{:S(2)}) collective-permute-start(bf16[192,128]{1,0:T(8,128)(2,1)S(1)} %bitcast.230), channel_id=1, source_target_pairs={{0,8},{8,16},{16,24},{1,9},{9,17},{17,25},{2,10},{10,18},{18,26},{... | collective-permute-start | bytes 147464 | tf_op jit(solution)/shard_map/ppermute | solution.py:53
  102.2 38.0 %slice-start = ((s8[8388608]{0:T(1024)(128)(4,1)}), s8[4194304]{0:T(1024)(128)(4,1)S(1)}, s32[]{:S(2)}) async-start(s8[8388608]{0:T(1024)(128)(4,1)} %bitcast.193), calls=%async_computation.2 | async-start | bytes 8388608
  103.4 36.8 %slice-start.1 = ((s8[8388608]{0:T(1024)(128)(4,1)}), s8[4194304]{0:T(1024)(128)(4,1)S(1)}, s32[]{:S(2)}) async-start(s8[8388608]{0:T(1024)(128)(4,1)} %bitcast.193), calls=%async_computation.3 | async-start | bytes 8388608
  103.9 6.0 %collective-permute-start.24 = (bf16[256,128]{1,0:T(8,128)(2,1)S(1)}, bf16[256,128]{1,0:T(8,128)(2,1)S(1)}, u32[]{:S(2)}, u32[]{:S(2)}) collective-permute-start(bf16[256,128]{1,0:T(8,128)(2,1)S(1)} %get-tuple-element.80), channel_id=1, source_target_pairs={{0,1},{1,2},{2,3},{3,4},{4,5},{5,6},{6,7},{7,0},{8,9},{9,10},{10,1... | collective-permute-start | bytes 196616 | tf_op jit(solution)/shard_map/ppermute | solution.py:24
  105.5 4.5 %collective-permute-start.25 = (bf16[256,128]{1,0:T(8,128)(2,1)S(1)}, bf16[256,128]{1,0:T(8,128)(2,1)S(1)}, u32[]{:S(2)}, u32[]{:S(2)}) collective-permute-start(bf16[256,128]{1,0:T(8,128)(2,1)S(1)} %get-tuple-element.81), channel_id=1, source_target_pairs={{0,7},{1,0},{2,1},{3,2},{4,3},{5,4},{6,5},{7,6},{8,15},{9,8},{10,9... | collective-permute-start | bytes 196616 | tf_op jit(solution)/shard_map/ppermute | solution.py:24
  110.0 7.5 %collective-permute-start.26 = (bf16[192,128]{1,0:T(8,128)(2,1)S(1)}, bf16[192,128]{1,0:T(8,128)(2,1)S(1)}, u32[]{:S(2)}, u32[]{:S(2)}) collective-permute-start(bf16[192,128]{1,0:T(8,128)(2,1)S(1)} %pad_maximum_fusion.9), channel_id=1, source_target_pairs={{0,3},{1,4},{2,5},{3,6},{4,7},{5,0},{6,1},{7,2},{8,11},{9,12},{10,... | collective-permute-start | bytes 147464 | tf_op jit(solution)/shard_map/ppermute | solution.py:24
  114.7 6.2 %collective-permute-start.27 = (bf16[128,128]{1,0:T(8,128)(2,1)S(1)}, bf16[128,128]{1,0:T(8,128)(2,1)S(1)}, u32[]{:S(2)}, u32[]{:S(2)}) collective-permute-start(bf16[128,128]{1,0:T(8,128)(2,1)S(1)} %pad_maximum_fusion.11), channel_id=1, source_target_pairs={{0,5},{1,6},{2,7},{3,0},{4,1},{5,2},{6,3},{7,4},{8,13},{9,14},{10,... | collective-permute-start | bytes 98312 | tf_op jit(solution)/shard_map/ppermute | solution.py:24
  121.1 11.5 %copy-start.6 = (bf16[256,2048]{1,0:T(8,128)(2,1)S(1)}, bf16[256,2048]{1,0:T(8,128)(2,1)}, u32[]{:S(2)}) copy-start(bf16[256,2048]{1,0:T(8,128)(2,1)} %get-tuple-element.5) | copy-start | bytes 3145732
  121.1 7.4 %collective-permute-start.29 = (bf16[704,128]{1,0:T(8,128)(2,1)S(1)}, bf16[704,128]{1,0:T(8,128)(2,1)S(1)}, u32[]{:S(2)}, u32[]{:S(2)}) collective-permute-start(bf16[704,128]{1,0:T(8,128)(2,1)S(1)} %get-tuple-element.69), channel_id=1, source_target_pairs={{0,24},{8,0},{16,8},{24,16},{1,25},{9,1},{17,9},{25,17},{2,26},{10... | collective-permute-start | bytes 540680 | tf_op jit(solution)/shard_map/ppermute | solution.py:24
  121.2 7.3 %collective-permute-start.30 = (bf16[512,128]{1,0:T(8,128)(2,1)S(1)}, bf16[512,128]{1,0:T(8,128)(2,1)S(1)}, u32[]{:S(2)}, u32[]{:S(2)}) collective-permute-start(bf16[512,128]{1,0:T(8,128)(2,1)S(1)} %constant_dynamic-slice_fusion.1), channel_id=1, source_target_pairs={{0,16},{8,24},{16,0},{24,8},{1,17},{9,25},{17,1},{25,9},{2,18},{10... | collective-permute-start | bytes 393224 | tf_op jit(solution)/shard_map/ppermute | solution.py:24
  122.5 7.8 %collective-permute-start.28 = (bf16[704,128]{1,0:T(8,128)(2,1)S(1)}, bf16[704,128]{1,0:T(8,128)(2,1)S(1)}, u32[]{:S(2)}, u32[]{:S(2)}) collective-permute-start(bf16[704,128]{1,0:T(8,128)(2,1)S(1)} %get-tuple-element.70), channel_id=1, source_target_pairs={{0,8},{8,16},{16,24},{24,0},{1,9},{9,17},{17,25},{25,1},{2,10},{10... | collective-permute-start | bytes 540680 | tf_op jit(solution)/shard_map/ppermute | solution.py:24
  130.3 2.6 %copy-start.5 = (bf16[256,2048]{1,0:T(8,128)(2,1)S(1)}, bf16[256,2048]{1,0:T(8,128)(2,1)}, u32[]{:S(2)}) copy-start(bf16[256,2048]{1,0:T(8,128)(2,1)} %get-tuple-element.4) | copy-start | bytes 3145732
  130.5 2.0 %collective-permute-start.31 = (bf16[2048,128]{1,0:T(8,128)(2,1)S(1)}, bf16[2048,128]{1,0:T(8,128)(2,1)S(1)}, u32[]{:S(2)}, u32[]{:S(2)}) collective-permute-start(bf16[2048,128]{1,0:T(8,128)(2,1)S(1)} %constant_dynamic-slice_fusion), channel_id=1, source_target_pairs={{0,32},{32,0},{1,33},{33,1},{2,34},{34,2},{3,35},{35,3},{4,36},{36... | collective-permute-start | bytes 1572872 | tf_op jit(solution)/shard_map/ppermute | solution.py:24
  130.7 9.5 %collective-permute-start.22 = (bf16[192,128]{1,0:T(8,128)(2,1)S(1)}, bf16[192,128]{1,0:T(8,128)(2,1)S(1)}, u32[]{:S(2)}, u32[]{:S(2)}) collective-permute-start(bf16[192,128]{1,0:T(8,128)(2,1)S(1)} %bitcast.228), channel_id=1, source_target_pairs={{0,32},{32,0},{1,33},{33,1},{2,34},{34,2},{3,35},{35,3},{4,36},{36... | collective-permute-start | bytes 147464 | tf_op jit(solution)/shard_map/ppermute | solution.py:24
  131.3 8.9 %collective-permute-start.23 = (bf16[192,128]{1,0:T(8,128)(2,1)S(1)}, bf16[192,128]{1,0:T(8,128)(2,1)S(1)}, u32[]{:S(2)}, u32[]{:S(2)}) collective-permute-start(bf16[192,128]{1,0:T(8,128)(2,1)S(1)} %bitcast.227), channel_id=1, source_target_pairs={{32,64},{96,128},{160,192},{64,32},{128,96},{192,160},{33,65},{97,... | collective-permute-start | bytes 147464 | tf_op jit(solution)/shard_map/ppermute | solution.py:40
  133.4 14.5 %collective-permute-start.32 = (f32[64,128]{1,0:T(8,128)S(1)}, f32[64,128]{1,0:T(8,128)S(1)}, u32[]{:S(2)}, u32[]{:S(2)}) collective-permute-start(f32[64,128]{1,0:T(8,128)S(1)} %get-tuple-element.66), channel_id=1, source_target_pairs={{0,192},{64,0},{128,64},{192,128},{1,193},{65,1},{129,65},{193,129... | collective-permute-start | bytes 98312 | tf_op jit(solution)/shard_map/ppermute | solution.py:24
  138.3 9.6 %collective-permute-start.34 = (f32[64,128]{1,0:T(8,128)S(1)}, f32[64,128]{1,0:T(8,128)S(1)}, u32[]{:S(2)}, u32[]{:S(2)}) collective-permute-start(f32[64,128]{1,0:T(8,128)S(1)} %get-tuple-element.67), channel_id=1, source_target_pairs={{0,64},{64,128},{128,192},{192,0},{1,65},{65,129},{129,193},{193,1... | collective-permute-start | bytes 98312 | tf_op jit(solution)/shard_map/ppermute | solution.py:24
  138.3 9.6 %collective-permute-start.33 = (f32[64,128]{1,0:T(8,128)S(1)}, f32[64,128]{1,0:T(8,128)S(1)}, u32[]{:S(2)}, u32[]{:S(2)}) collective-permute-start(f32[64,128]{1,0:T(8,128)S(1)} %get-tuple-element.68), channel_id=1, source_target_pairs={{0,128},{64,192},{128,0},{192,64},{1,129},{65,193},{129,1},{193,65... | collective-permute-start | bytes 98312 | tf_op jit(solution)/shard_map/ppermute | solution.py:24
  149.1 11.3 %collective-permute-start.36 = (bf16[192,128]{1,0:T(8,128)(2,1)S(1)}, bf16[192,128]{1,0:T(8,128)(2,1)S(1)}, u32[]{:S(2)}, u32[]{:S(2)}) collective-permute-start(bf16[192,128]{1,0:T(8,128)(2,1)S(1)} %bitcast.226), channel_id=1, source_target_pairs={{0,32},{32,0},{1,33},{33,1},{2,34},{34,2},{3,35},{35,3},{4,36},{36... | collective-permute-start | bytes 147464 | tf_op jit(solution)/shard_map/ppermute | solution.py:24
  149.2 13.4 %collective-permute-start.35 = (bf16[192,128]{1,0:T(8,128)(2,1)S(1)}, bf16[192,128]{1,0:T(8,128)(2,1)S(1)}, u32[]{:S(2)}, u32[]{:S(2)}) collective-permute-start(bf16[192,128]{1,0:T(8,128)(2,1)S(1)} %bitcast.224), channel_id=1, source_target_pairs={{32,64},{96,128},{160,192},{64,32},{128,96},{192,160},{33,65},{97,... | collective-permute-start | bytes 147464 | tf_op jit(solution)/shard_map/ppermute | solution.py:40
  150.0 12.7 %collective-permute-start.38 = (bf16[192,128]{1,0:T(8,128)(2,1)S(1)}, bf16[192,128]{1,0:T(8,128)(2,1)S(1)}, u32[]{:S(2)}, u32[]{:S(2)}) collective-permute-start(bf16[192,128]{1,0:T(8,128)(2,1)S(1)} %bitcast.239), channel_id=1, source_target_pairs={{8,0},{16,8},{24,16},{9,1},{17,9},{25,17},{10,2},{18,10},{26,18},{... | collective-permute-start | bytes 147464 | tf_op jit(solution)/shard_map/ppermute | solution.py:54
  153.7 9.1 %collective-permute-start.40 = (bf16[192,128]{1,0:T(8,128)(2,1)S(1)}, bf16[192,128]{1,0:T(8,128)(2,1)S(1)}, u32[]{:S(2)}, u32[]{:S(2)}) collective-permute-start(bf16[192,128]{1,0:T(8,128)(2,1)S(1)} %bitcast.233), channel_id=1, source_target_pairs={{1,0},{2,1},{3,2},{4,3},{5,4},{6,5},{7,6},{9,8},{10,9},{11,10},{12... | collective-permute-start | bytes 147464 | tf_op jit(solution)/shard_map/ppermute | solution.py:54
  155.0 7.9 %collective-permute-start.39 = (bf16[192,128]{1,0:T(8,128)(2,1)S(1)}, bf16[192,128]{1,0:T(8,128)(2,1)S(1)}, u32[]{:S(2)}, u32[]{:S(2)}) collective-permute-start(bf16[192,128]{1,0:T(8,128)(2,1)S(1)} %bitcast.231), channel_id=1, source_target_pairs={{0,1},{1,2},{2,3},{3,4},{4,5},{5,6},{6,7},{8,9},{9,10},{10,11},{11... | collective-permute-start | bytes 147464 | tf_op jit(solution)/shard_map/ppermute | solution.py:53
  160.2 6.4 %copy-start.8 = (f32[3,8,8,8,128]{4,3,2,1,0:T(8,128)S(1)}, f32[3,8,8,8,128]{4,3,2,1,0:T(8,128)}, u32[]{:S(2)}) copy-start(f32[3,8,8,8,128]{4,3,2,1,0:T(8,128)} %param.7) | copy-start | bytes 2359300
  160.5 6.0 %collective-permute-start.37 = (bf16[192,128]{1,0:T(8,128)(2,1)S(1)}, bf16[192,128]{1,0:T(8,128)(2,1)S(1)}, u32[]{:S(2)}, u32[]{:S(2)}) collective-permute-start(bf16[192,128]{1,0:T(8,128)(2,1)S(1)} %bitcast.229), channel_id=1, source_target_pairs={{0,8},{8,16},{16,24},{1,9},{9,17},{17,25},{2,10},{10,18},{18,26},{... | collective-permute-start | bytes 147464 | tf_op jit(solution)/shard_map/ppermute | solution.py:53
where the time goes:
time: 200 us; the launch traced here: 198 us
  starting transfers between devices  72.2 us (36%)
  waiting for transfers between devices  38 us (19%)
  blocking collectives  27.3 us (14%)
  local copies, waits for them, and re-layouts  24.3 us (12%)
  Pallas kernels  19 us (10%)
  other arithmetic  9.84 us (5%)
  matrix products  5.36 us (3%)
    ppermute x29, starting transfers between devices, shift(): lax.ppermute(value, axis, [(i, (i + step) % count) for i in range(count)])  45.2 us
    ppermute x29, waiting for transfers between devices, shift(): lax.ppermute(value, axis, [(i, (i + step) % count) for i in range(count)])  30.5 us
    all_to_all x2, blocking collectives, everywhere(): partial = jnp.sum(lax.all_to_all(copies, axes, 0, 0, tiled=True), axis=0)  27.3 us
    pallas_call x2, Pallas kernels, local_solve(): pl.pallas_call(local_kernel, out_shape=jax.ShapeDtypeStruct(own.shape, jn...  15.3 us
    ppermute x4, starting transfers between devices, halo(): faces.append(lax.ppermute(last, axis, up))  13.2 us
    unnamed x76, local copies, waits for them, and re-layouts  11.8 us
    ppermute x4, starting transfers between devices, halo(): faces.append(lax.ppermute(first, axis, [(b, a) for a, b in up]))  11.2 us
    ppermute x4, waiting for transfers between devices, halo(): faces.append(lax.ppermute(last, axis, up))  7.45 us
  transfers between devices with their start and end apart: 41, of which 14 were waited for; matrix products, arithmetic and copies ran while one was open for 9% of the time, Pallas kernels for 10%

commit v1 on v0

--- a/solution.py
+++ b/solution.py
@@ -193,44 +193,37 @@
 def stack_kernel(place, *refs):
     pieces, (mine, theirs) = refs[:-2], refs[-2:]
     rows, width = pieces[0].shape[0], mine.shape[1]
-    for core, out in ((place[1], mine), (1 - place[1], theirs)):
+    for core, out in ((place[0], mine), (1 - place[0], theirs)):
         columns = pl.ds(pl.multiple_of(core * width, width), width)
         for step, piece in enumerate(pieces):
             out[pl.ds(step * rows, rows)] = piece[:, columns]
 
 
-def stack(coarse_inverse, pieces):
+def stack(place, pieces):
     rows, width = pieces[0].shape
-    count = len(pieces) + 1
-    place = jnp.stack([lax.axis_index(X), lax.axis_index(C)]).astype(jnp.int32)
-    whole = pl.BlockSpec((rows, width), lambda i, place: (0, 0))
-    result = pl.BlockSpec((rows * count, width // 2), lambda i, place: (0, 0))
-    shape = jax.ShapeDtypeStruct((rows * count, width // 2), coarse_inverse.dtype)
+    vmem = pl.BlockSpec(memory_space=pltpu.VMEM)
+    shape = jax.ShapeDtypeStruct((rows * len(pieces), width // 2), pieces[0].dtype)
     return pl.pallas_call(
         stack_kernel,
         out_shape=(shape, shape),
-        grid_spec=pltpu.PrefetchScalarGridSpec(
-            num_scalar_prefetch=1,
-            grid=(1,),
-            in_specs=[pl.BlockSpec((rows, width), lambda i, place: (0, place[0]))]
-            + [whole] * len(pieces),
-            out_specs=(result, result),
-        ),
+        in_specs=[pl.BlockSpec(memory_space=pltpu.SMEM)] + [vmem] * len(pieces),
+        out_specs=(vmem, vmem),
+        compiler_params=pltpu.CompilerParams(vmem_limit_bytes=6 * 1024 * 1024),
         name="stack",
-    )(place, coarse_inverse, *pieces)
-
-
-def spread(coarse_inverse):
+    )(place, *pieces)
+
+
+def spread(place, coarse_inverse):
     rows, total = coarse_inverse.shape
     count = lax.axis_size(X)
     width = total // count
     at_x = lax.axis_index(X)
     pieces = []
-    for step in range(1, count):
-        place = (at_x + step) & (count - 1)
-        piece = lax.dynamic_slice(coarse_inverse, (0, place * width), (rows, width))
-        pieces.append(shift(piece, X, step))
-    return stack(coarse_inverse, pieces)
+    for step in range(count):
+        at = (at_x + step) & (count - 1)
+        piece = lax.dynamic_slice(coarse_inverse, (0, at * width), (rows, width))
+        pieces.append(shift(piece, X, step) if step else piece)
+    return stack(place, pieces)
 
 
 def rolled(value, start, rows):
@@ -301,8 +294,8 @@
             at_z < lax.axis_size(Z) - 1,
         ]
     ).astype(jnp.int32)
+    stacks = spread(place, coarse_inverse)
     diagonal = 6.0 + stiffness[..., None]
-    stacks = spread(coarse_inverse)
 
     def precondition(field):
         rounded = field.astype(jnp.bfloat16)

time: 200 us -> 196 us (0.980)
  local copies, waits for them, and re-layouts: 24.3 us -> 21.3 us
  Pallas kernels: 19 us -> 16.3 us
  other arithmetic: 9.84 us -> 7.61 us
  waiting for transfers between devices: 38 us -> 40 us
    pallas_call x1, Pallas kernels: 3.66 us -> 0.68 us  [stack(): pl.pallas_call(stack_kernel, out_shape=(shape, shape), in_specs=[pl.Block...]
    slice x6, local copies, waits for them, and re-layouts: 2.49 us -> 0.35 us  [ends(): first = lax.slice_in_dim(blocks, 0, 1, axis=dim).reshape(-1, lanes)]
    ppermute x29, waiting for transfers between devices: 30.5 us -> 32.5 us  [shift(): lax.ppermute(value, axis, [(i, (i + step) % count) for i in range(count)])]
    unnamed x76 -> x92, local copies, waits for them, and re-layouts: 11.8 us -> 11.1 us
  transfers between devices with their start and end apart: 41 -> 41, of which waited for: 14 -> 15; matrix products, arithmetic and copies ran while one was open for 9% -> 7% of each run, Pallas kernels for 10% -> 8%
where the time goes in v1:
time: 196 us; the launch traced here: 194 us
  starting transfers between devices  73.9 us (38%)
  waiting for transfers between devices  40 us (20%)
  blocking collectives  26.7 us (14%)
  local copies, waits for them, and re-layouts  21.3 us (11%)
  Pallas kernels  16.3 us (8%)
  other arithmetic  7.61 us (4%)
  matrix products  5.77 us (3%)
  between operations  1.98 us (1%)
    ppermute x29, starting transfers between devices, shift(): lax.ppermute(value, axis, [(i, (i + step) % count) for i in range(count)])  46.3 us
    ppermute x29, waiting for transfers between devices, shift(): lax.ppermute(value, axis, [(i, (i + step) % count) for i in range(count)])  32.5 us
    all_to_all x2, blocking collectives, everywhere(): partial = jnp.sum(lax.all_to_all(copies, axes, 0, 0, tiled=True), axis=0)  26.7 us
    pallas_call x2, Pallas kernels, local_solve(): pl.pallas_call(local_kernel, out_shape=jax.ShapeDtypeStruct(own.shape, jn...  15.7 us
    ppermute x4, starting transfers between devices, halo(): faces.append(lax.ppermute(last, axis, up))  13.2 us
    ppermute x4, starting transfers between devices, halo(): faces.append(lax.ppermute(first, axis, [(b, a) for a, b in up]))  11.2 us
    unnamed x92, local copies, waits for them, and re-layouts  11.1 us
    ppermute x4, waiting for transfers between devices, halo(): faces.append(lax.ppermute(last, axis, up))  7.47 us
  transfers between devices with their start and end apart: 41, of which 15 were waited for; matrix products, arithmetic and copies ran while one was open for 7% of the time, Pallas kernels for 8%

profile of v1, /device:TPU:8, one launch (start us, length us, event | category | flops | bytes accessed | tf_op | source)
XLA Modules:
  0.0 193.6 jit_solution(4285121161194001371)
XLA Ops:
  0.7 1.4 fusion.8
  2.8 2.0 %collective-permute-start.2 = (bf16[256,128]{1,0:T(8,128)(2,1)S(1)}, bf16[256,128]{1,0:T(8,128)(2,1)S(1)}, u32[]{:S(2)}, u32[]{:S(2)}) collective-permute-start(bf16[256,128]{1,0:T(8,128)(2,1)S(1)} %get-tuple-element.83), channel_id=1, source_target_pairs={{0,1},{1,2},{2,3},{3,4},{4,5},{5,6},{6,7},{7,0},{8,9},{9,10},{10,1... | collective-permute-start | bytes 196616 | tf_op jit(solution)/shard_map/ppermute | solution.py:24
  4.7 4.0 %collective-permute-start.3 = (bf16[256,128]{1,0:T(8,128)(2,1)S(1)}, bf16[256,128]{1,0:T(8,128)(2,1)S(1)}, u32[]{:S(2)}, u32[]{:S(2)}) collective-permute-start(bf16[256,128]{1,0:T(8,128)(2,1)S(1)} %get-tuple-element.84), channel_id=1, source_target_pairs={{0,7},{1,0},{2,1},{3,2},{4,3},{5,4},{6,5},{7,6},{8,15},{9,8},{10,9... | collective-permute-start | bytes 196616 | tf_op jit(solution)/shard_map/ppermute | solution.py:24
  9.0 1.9 %collective-permute-done.2.rest_4_ = bf16[256,128]{1,0:T(8,128)(2,1)S(1)} collective-permute-done((bf16[256,128]{1,0:T(8,128)(2,1)S(1)}, bf16[256,128]{1,0:T(8,128)(2,1)S(1)}, u32[]{:S(2)}, u32[]{:S(2)}) %collective-permute-start.2) | collective-permute-done | bytes 65568 | tf_op jit(solution)/shard_map/ppermute | solution.py:24
  10.9 5.2 %collective-permute-start.4 = (bf16[192,128]{1,0:T(8,128)(2,1)S(1)}, bf16[192,128]{1,0:T(8,128)(2,1)S(1)}, u32[]{:S(2)}, u32[]{:S(2)}) collective-permute-start(bf16[192,128]{1,0:T(8,128)(2,1)S(1)} %pad_maximum_fusion.8), channel_id=1, source_target_pairs={{0,3},{1,4},{2,5},{3,6},{4,7},{5,0},{6,1},{7,2},{8,11},{9,12},{10,... | collective-permute-start | bytes 147464 | tf_op jit(solution)/shard_map/ppermute | solution.py:24
  16.1 2.1 %collective-permute-done.4 = bf16[192,128]{1,0:T(8,128)(2,1)S(1)} collective-permute-done((bf16[192,128]{1,0:T(8,128)(2,1)S(1)}, bf16[192,128]{1,0:T(8,128)(2,1)S(1)}, u32[]{:S(2)}, u32[]{:S(2)}) %collective-permute-start.4) | collective-permute-done | bytes 49184 | tf_op jit(solution)/shard_map/ppermute | solution.py:24
  18.2 3.6 %collective-permute-done.5 = bf16[128,128]{1,0:T(8,128)(2,1)S(1)} collective-permute-done((bf16[128,128]{1,0:T(8,128)(2,1)S(1)}, bf16[128,128]{1,0:T(8,128)(2,1)S(1)}, u32[]{:S(2)}, u32[]{:S(2)}) %collective-permute-start.5) | collective-permute-done | bytes 32800 | tf_op jit(solution)/shard_map/ppermute | solution.py:24
  22.0 0.8 pad_maximum_fusion
  23.2 2.7 %constant_dynamic-slice_fusion.3 = (bf16[64,4096]{1,0:T(8,128)(2,1)}, bf16[64,4096]{1,0:T(8,128)(2,1)}, bf16[64,4096]{1,0:T(8,128)(2,1)S(1)}, bf16[64,4096]{1,0:T(8,128)(2,1)}) fusion(bf16[64,16384]{1,0:T(8,128)(2,1)} %param.13, s32[]{:T(128)S(6)} %select_n.107, s32[]{:T(128)S(6)} %select_n.105, s32[]{:T(128)S(6)} %select_n.104, s32[]{:T(128)S(6)} %select_n.106), kind=kLoop, calls=%fused_computation.105 | loop fusion | bytes 4194320 | tf_op jit(solution)/shard_map/dynamic_slice | solution.py:224
  25.9 2.8 %collective-permute-start.10 = (bf16[64,4096]{1,0:T(8,128)(2,1)}, bf16[64,4096]{1,0:T(8,128)(2,1)S(1)}, u32[]{:S(2)}, u32[]{:S(2)}) collective-permute-start(bf16[64,4096]{1,0:T(8,128)(2,1)} %get-tuple-element.27), channel_id=1, source_target_pairs={{0,192},{64,0},{128,64},{192,128},{1,193},{65,1},{129,65},{193,129... | collective-permute-start | bytes 1572872 | tf_op jit(solution)/shard_map/ppermute | solution.py:24
  28.7 2.3 %collective-permute-start.9 = (bf16[64,4096]{1,0:T(8,128)(2,1)}, bf16[64,4096]{1,0:T(8,128)(2,1)S(1)}, u32[]{:S(2)}, u32[]{:S(2)}) collective-permute-start(bf16[64,4096]{1,0:T(8,128)(2,1)} %get-tuple-element.30), channel_id=1, source_target_pairs={{0,128},{64,192},{128,0},{192,64},{1,129},{65,193},{129,1},{193,65... | collective-permute-start | bytes 1572872 | tf_op jit(solution)/shard_map/ppermute | solution.py:24
  30.9 2.6 %collective-permute-start.11 = (bf16[512,128]{1,0:T(8,128)(2,1)}, bf16[512,128]{1,0:T(8,128)(2,1)S(1)}, u32[]{:S(2)}, u32[]{:S(2)}) collective-permute-start(bf16[512,128]{1,0:T(8,128)(2,1)} %copy-done.18), channel_id=1, source_target_pairs={{0,16},{8,24},{16,0},{24,8},{1,17},{9,25},{17,1},{25,9},{2,18},{10... | collective-permute-start | bytes 393224 | tf_op jit(solution)/shard_map/ppermute | solution.py:24
  33.5 1.9 collective-permute-start.6
  35.4 2.2 %collective-permute-done.11 = bf16[512,128]{1,0:T(8,128)(2,1)S(1)} collective-permute-done((bf16[512,128]{1,0:T(8,128)(2,1)}, bf16[512,128]{1,0:T(8,128)(2,1)S(1)}, u32[]{:S(2)}, u32[]{:S(2)}) %collective-permute-start.11) | collective-permute-done | bytes 131104 | tf_op jit(solution)/shard_map/ppermute | solution.py:24
  37.7 2.0 %collective-permute-done.6.rest_2_ = bf16[704,128]{1,0:T(8,128)(2,1)S(1)} collective-permute-done((bf16[704,128]{1,0:T(8,128)(2,1)}, bf16[704,128]{1,0:T(8,128)(2,1)S(1)}, u32[]{:S(2)}, u32[]{:S(2)}) %collective-permute-start.6) | collective-permute-done | bytes 180256 | tf_op jit(solution)/shard_map/ppermute | solution.py:24
  39.9 0.8 constant_dynamic-slice_fusion.2
  40.7 0.8 broadcast_select_fusion.10
  43.4 4.9 %collective-permute-done.10.refs_3_ = bf16[64,4096]{1,0:T(8,128)(2,1)S(1)} collective-permute-done((bf16[64,4096]{1,0:T(8,128)(2,1)}, bf16[64,4096]{1,0:T(8,128)(2,1)S(1)}, u32[]{:S(2)}, u32[]{:S(2)}) %collective-permute-start.10) | collective-permute-done | bytes 524320 | tf_op jit(solution)/shard_map/ppermute | solution.py:24
  48.3 0.8 copy-done.4
  49.1 1.3 collective-permute-start.1
  50.4 1.2 collective-permute-done.8.refs_1_
  51.6 0.8 copy-done.6
  52.4 0.8 copy-done.8
  53.2 1.0 copy-done.5
  54.2 1.0 copy-done.7
  55.3 1.0 copy-done.9
  56.3 0.7 stack.73
  57.0 1.5 fusion.58
  58.6 1.5 convolution_add_fusion.1
  60.7 3.0 %collective-permute-start.13 = (f32[64,128]{1,0:T(8,128)}, f32[64,128]{1,0:T(8,128)S(1)}, u32[]{:S(2)}, u32[]{:S(2)}) collective-permute-start(f32[64,128]{1,0:T(8,128)} %get-tuple-element.72), channel_id=1, source_target_pairs={{0,192},{64,0},{128,64},{192,128},{1,193},{65,1},{129,65},{193,129... | collective-permute-start | bytes 98312 | tf_op jit(solution)/shard_map/ppermute | solution.py:24
  63.7 1.5 collective-permute-start.14
  65.3 0.7 copy.135
  66.2 3.4 %copy-done.1 = bf16[1,1,1,2048,2048]{4,3,2,1,0:T(8,128)(2,1)S(1)} copy-done((bf16[1,1,1,2048,2048]{4,3,2,1,0:T(8,128)(2,1)S(1)}, bf16[1,1,1,2048,2048]{4,3,2,1,0:T(8,128)(2,1)}, u32[]{:S(2)}) %copy-start.1) | copy-done | bytes 8388632
  69.6 8.0 %local_solve.2 = f32[1536,128]{1,0:T(8,128)S(1)} custom-call(s32[5]{0:T(128)S(1)} %stack.62.place, s32[512,1]{1,0:T(8,128)S(1)} %copy.141.order, bf16[1536,128]{1,0:T(8,128)(2,1)S(1)} %bitcast.196, bf16[192,128]{1,0:T(8,128)(2,1)} %collective-permute-done.rest_0_, bf16[192,128]{1,0:T(8,128)(2,1)} %collective-permute-done.1.rest_1_, ...), custom_call_target="tpu_custom_call" | custom-call | tf_op jit(solution)/shard_map/local_solve/pallas_call | solution.py:174
  77.7 1.1 fusion.17
  79.6 1.4 collective-permute-start.17
  81.7 4.9 %collective-permute-start.19 = (bf16[192,128]{1,0:T(8,128)(2,1)S(1)}, bf16[192,128]{1,0:T(8,128)(2,1)S(1)}, u32[]{:S(2)}, u32[]{:S(2)}) collective-permute-start(bf16[192,128]{1,0:T(8,128)(2,1)S(1)} %bitcast.240), channel_id=1, source_target_pairs={{8,0},{16,8},{24,16},{9,1},{17,9},{25,17},{10,2},{18,10},{26,18},{... | collective-permute-start | bytes 147464 | tf_op jit(solution)/shard_map/ppermute | solution.py:54
  86.7 1.3 collective-permute-start.21
  88.0 4.5 %collective-permute-start.20 = (bf16[192,128]{1,0:T(8,128)(2,1)S(1)}, bf16[192,128]{1,0:T(8,128)(2,1)S(1)}, u32[]{:S(2)}, u32[]{:S(2)}) collective-permute-start(bf16[192,128]{1,0:T(8,128)(2,1)S(1)} %bitcast.231), channel_id=1, source_target_pairs={{0,1},{1,2},{2,3},{3,4},{4,5},{5,6},{6,7},{8,9},{9,10},{10,11},{11... | collective-permute-start | bytes 147464 | tf_op jit(solution)/shard_map/ppermute | solution.py:53
  93.4 1.9 collective-permute-start.18
  95.6 3.8 %collective-permute-done.18 = bf16[192,128]{1,0:T(8,128)(2,1)S(1)} collective-permute-done((bf16[192,128]{1,0:T(8,128)(2,1)S(1)}, bf16[192,128]{1,0:T(8,128)(2,1)S(1)}, u32[]{:S(2)}, u32[]{:S(2)}) %collective-permute-start.18) | collective-permute-done | bytes 49184 | tf_op jit(solution)/shard_map/ppermute | solution.py:53
  101.2 1.6 collective-permute-start.24
  102.8 1.7 collective-permute-start.25
  104.7 2.5 %collective-permute-done.24.rest_4_ = bf16[256,128]{1,0:T(8,128)(2,1)S(1)} collective-permute-done((bf16[256,128]{1,0:T(8,128)(2,1)S(1)}, bf16[256,128]{1,0:T(8,128)(2,1)S(1)}, u32[]{:S(2)}, u32[]{:S(2)}) %collective-permute-start.24) | collective-permute-done | bytes 65568 | tf_op jit(solution)/shard_map/ppermute | solution.py:24
  107.2 3.6 %collective-permute-start.26 = (bf16[192,128]{1,0:T(8,128)(2,1)S(1)}, bf16[192,128]{1,0:T(8,128)(2,1)S(1)}, u32[]{:S(2)}, u32[]{:S(2)}) collective-permute-start(bf16[192,128]{1,0:T(8,128)(2,1)S(1)} %pad_maximum_fusion.9), channel_id=1, source_target_pairs={{0,3},{1,4},{2,5},{3,6},{4,7},{5,0},{6,1},{7,2},{8,11},{9,12},{10,... | collective-permute-start | bytes 147464 | tf_op jit(solution)/shard_map/ppermute | solution.py:24
  110.8 1.5 collective-permute-start.27
  112.4 2.6 %collective-permute-done.26 = bf16[192,128]{1,0:T(8,128)(2,1)S(1)} collective-permute-done((bf16[192,128]{1,0:T(8,128)(2,1)S(1)}, bf16[192,128]{1,0:T(8,128)(2,1)S(1)}, u32[]{:S(2)}, u32[]{:S(2)}) %collective-permute-start.26) | collective-permute-done | bytes 49184 | tf_op jit(solution)/shard_map/ppermute | solution.py:24
  115.0 2.4 %collective-permute-done.27 = bf16[128,128]{1,0:T(8,128)(2,1)S(1)} collective-permute-done((bf16[128,128]{1,0:T(8,128)(2,1)S(1)}, bf16[128,128]{1,0:T(8,128)(2,1)S(1)}, u32[]{:S(2)}, u32[]{:S(2)}) %collective-permute-start.27) | collective-permute-done | bytes 32800 | tf_op jit(solution)/shard_map/ppermute | solution.py:24
  117.6 1.3 collective-permute-start.30
  118.9 1.2 collective-permute-start.28
  120.2 5.2 %collective-permute-done.29.rest_3_ = bf16[704,128]{1,0:T(8,128)(2,1)S(1)} collective-permute-done((bf16[704,128]{1,0:T(8,128)(2,1)S(1)}, bf16[704,128]{1,0:T(8,128)(2,1)S(1)}, u32[]{:S(2)}, u32[]{:S(2)}) %collective-permute-start.29) | collective-permute-done | bytes 180256 | tf_op jit(solution)/shard_map/ppermute | solution.py:24
  125.4 1.2 collective-permute-done.28.rest_2_
  129.7 5.1 %collective-permute-start.32 = (f32[64,128]{1,0:T(8,128)S(1)}, f32[64,128]{1,0:T(8,128)S(1)}, u32[]{:S(2)}, u32[]{:S(2)}) collective-permute-start(f32[64,128]{1,0:T(8,128)S(1)} %get-tuple-element.67), channel_id=1, source_target_pairs={{0,192},{64,0},{128,64},{192,128},{1,193},{65,1},{129,65},{193,129... | collective-permute-start | bytes 98312 | tf_op jit(solution)/shard_map/ppermute | solution.py:24
  134.9 1.8 collective-permute-start.33
  136.7 7.7 %local_solve.3 = f32[1536,128]{1,0:T(8,128)S(1)} custom-call(s32[5]{0:T(128)S(1)} %stack.62.place, s32[512,1]{1,0:T(8,128)S(1)} %copy.141.order, bf16[1536,128]{1,0:T(8,128)(2,1)S(1)} %get-tuple-element.25.own, bf16[192,128]{1,0:T(8,128)(2,1)S(1)} %collective-permute-done.22.rest_0_, bf16[192,128]{1,0:T(8,128)(2,1)S(1)} %collective-permute-done.23.rest_1_, ...), custom_call_target="tpu_custom_call" | custom-call | tf_op jit(solution)/shard_map/local_solve/pallas_call | solution.py:174
  146.4 3.7 %collective-permute-start.38 = (bf16[192,128]{1,0:T(8,128)(2,1)S(1)}, bf16[192,128]{1,0:T(8,128)(2,1)S(1)}, u32[]{:S(2)}, u32[]{:S(2)}) collective-permute-start(bf16[192,128]{1,0:T(8,128)(2,1)S(1)} %bitcast.238), channel_id=1, source_target_pairs={{8,0},{16,8},{24,16},{9,1},{17,9},{25,17},{10,2},{18,10},{26,18},{... | collective-permute-start | bytes 147464 | tf_op jit(solution)/shard_map/ppermute | solution.py:54
  150.2 1.3 collective-permute-start.40
  151.5 4.5 %collective-permute-start.39 = (bf16[192,128]{1,0:T(8,128)(2,1)S(1)}, bf16[192,128]{1,0:T(8,128)(2,1)S(1)}, u32[]{:S(2)}, u32[]{:S(2)}) collective-permute-start(bf16[192,128]{1,0:T(8,128)(2,1)S(1)} %bitcast.230), channel_id=1, source_target_pairs={{0,1},{1,2},{2,3},{3,4},{4,5},{5,6},{6,7},{8,9},{9,10},{10,11},{11... | collective-permute-start | bytes 147464 | tf_op jit(solution)/shard_map/ppermute | solution.py:53
  156.9 2.1 %collective-permute-start.37 = (bf16[192,128]{1,0:T(8,128)(2,1)S(1)}, bf16[192,128]{1,0:T(8,128)(2,1)S(1)}, u32[]{:S(2)}, u32[]{:S(2)}) collective-permute-start(bf16[192,128]{1,0:T(8,128)(2,1)S(1)} %bitcast.228), channel_id=1, source_target_pairs={{0,8},{8,16},{16,24},{1,9},{9,17},{17,25},{2,10},{10,18},{18,26},{... | collective-permute-start | bytes 147464 | tf_op jit(solution)/shard_map/ppermute | solution.py:53
  159.3 3.6 %collective-permute-done.37 = bf16[192,128]{1,0:T(8,128)(2,1)S(1)} collective-permute-done((bf16[192,128]{1,0:T(8,128)(2,1)S(1)}, bf16[192,128]{1,0:T(8,128)(2,1)S(1)}, u32[]{:S(2)}, u32[]{:S(2)}) %collective-permute-start.37) | collective-permute-done | bytes 49184 | tf_op jit(solution)/shard_map/ppermute | solution.py:53
  163.0 1.4 multiply_reduce_fusion.2
  165.2 13.2 %all_to_all.10 = f32[16,6,128]{2,1,0:T(8,128)S(1)} all-to-all(f32[16,6,128]{2,1,0:T(8,128)S(1)} %broadcast_in_dim.4), channel_id=1, replica_groups=mesh['gx_0'=4,'gx_1'=2,'gy_0'=2,'gy_1'=2,'gz'=8] {'gx_0','gx_1','gy_1'}, dimensions={0} | all-to-all | bytes 98304 | tf_op jit(solution)/shard_map/all_to_all | solution.py:271
  178.5 13.5 %all_to_all.11 = f32[16,6,128]{2,1,0:T(8,128)S(1)} all-to-all(f32[16,6,128]{2,1,0:T(8,128)S(1)} %broadcast_in_dim.5), channel_id=1, replica_groups=mesh['gx_0'=4,'gx_1'=2,'gy_0'=2,'gy_1'=2,'gz'=8] {'gy_0','gz'}, dimensions={0} | all-to-all | bytes 98304 | tf_op jit(solution)/shard_map/all_to_all | solution.py:271
  192.6 1.0 multiply_add_fusion
  (221 shorter events, 16.5 us)
Async XLA Ops:
  0.6 1.7 copy-start
  0.6 1.7 copy-start.21
  2.0 20.7 %copy-start.14 = (bf16[3,8,8,8,128]{4,2,1,0,3:T(8,128)(2,1)}, bf16[3,8,8,8,128]{4,2,1,0,3:T(8,128)(2,1)S(1)}, u32[]{:S(2)}) copy-start(bf16[3,8,8,8,128]{4,2,1,0,3:T(8,128)(2,1)S(1)} %fusion.8) | copy-start | bytes 1179652
  2.5 23.4 %copy-start.12 = (bf16[64,1536]{1,0:T(8,128)(2,1)}, bf16[64,1536]{1,0:T(8,128)(2,1)S(1)}, u32[]{:S(2)}) copy-start(bf16[64,1536]{1,0:T(8,128)(2,1)S(1)} %convolution_convert_fusion) | copy-start | bytes 589828
  2.8 8.2 %collective-permute-start.2 = (bf16[256,128]{1,0:T(8,128)(2,1)S(1)}, bf16[256,128]{1,0:T(8,128)(2,1)S(1)}, u32[]{:S(2)}, u32[]{:S(2)}) collective-permute-start(bf16[256,128]{1,0:T(8,128)(2,1)S(1)} %get-tuple-element.83), channel_id=1, source_target_pairs={{0,1},{1,2},{2,3},{3,4},{4,5},{5,6},{6,7},{7,0},{8,9},{9,10},{10,1... | collective-permute-start | bytes 196616 | tf_op jit(solution)/shard_map/ppermute | solution.py:24
  4.7 6.2 %collective-permute-start.3 = (bf16[256,128]{1,0:T(8,128)(2,1)S(1)}, bf16[256,128]{1,0:T(8,128)(2,1)S(1)}, u32[]{:S(2)}, u32[]{:S(2)}) collective-permute-start(bf16[256,128]{1,0:T(8,128)(2,1)S(1)} %get-tuple-element.84), channel_id=1, source_target_pairs={{0,7},{1,0},{2,1},{3,2},{4,3},{5,4},{6,5},{7,6},{8,15},{9,8},{10,9... | collective-permute-start | bytes 196616 | tf_op jit(solution)/shard_map/ppermute | solution.py:24
  10.9 7.2 %collective-permute-start.4 = (bf16[192,128]{1,0:T(8,128)(2,1)S(1)}, bf16[192,128]{1,0:T(8,128)(2,1)S(1)}, u32[]{:S(2)}, u32[]{:S(2)}) collective-permute-start(bf16[192,128]{1,0:T(8,128)(2,1)S(1)} %pad_maximum_fusion.8), channel_id=1, source_target_pairs={{0,3},{1,4},{2,5},{3,6},{4,7},{5,0},{6,1},{7,2},{8,11},{9,12},{10,... | collective-permute-start | bytes 147464 | tf_op jit(solution)/shard_map/ppermute | solution.py:24
  16.1 5.7 %collective-permute-start.5 = (bf16[128,128]{1,0:T(8,128)(2,1)S(1)}, bf16[128,128]{1,0:T(8,128)(2,1)S(1)}, u32[]{:S(2)}, u32[]{:S(2)}) collective-permute-start(bf16[128,128]{1,0:T(8,128)(2,1)S(1)} %pad_maximum_fusion.10), channel_id=1, source_target_pairs={{0,5},{1,6},{2,7},{3,0},{4,1},{5,2},{6,3},{7,4},{8,13},{9,14},{10,... | collective-permute-start | bytes 98312 | tf_op jit(solution)/shard_map/ppermute | solution.py:24
  22.7 10.8 %collective-permute-start.7 = (bf16[704,128]{1,0:T(8,128)(2,1)}, bf16[704,128]{1,0:T(8,128)(2,1)S(1)}, u32[]{:S(2)}, u32[]{:S(2)}) collective-permute-start(bf16[704,128]{1,0:T(8,128)(2,1)} %get-tuple-element.75), channel_id=1, source_target_pairs={{0,24},{8,0},{16,8},{24,16},{1,25},{9,1},{17,9},{25,17},{2,26},{10... | collective-permute-start | bytes 540680 | tf_op jit(solution)/shard_map/ppermute | solution.py:24
  25.9 22.4 %collective-permute-start.10 = (bf16[64,4096]{1,0:T(8,128)(2,1)}, bf16[64,4096]{1,0:T(8,128)(2,1)S(1)}, u32[]{:S(2)}, u32[]{:S(2)}) collective-permute-start(bf16[64,4096]{1,0:T(8,128)(2,1)} %get-tuple-element.27), channel_id=1, source_target_pairs={{0,192},{64,0},{128,64},{192,128},{1,193},{65,1},{129,65},{193,129... | collective-permute-start | bytes 1572872 | tf_op jit(solution)/shard_map/ppermute | solution.py:24
  28.6 22.9 %collective-permute-start.8 = (bf16[64,4096]{1,0:T(8,128)(2,1)}, bf16[64,4096]{1,0:T(8,128)(2,1)S(1)}, u32[]{:S(2)}, u32[]{:S(2)}) collective-permute-start(bf16[64,4096]{1,0:T(8,128)(2,1)} %get-tuple-element.28), channel_id=1, source_target_pairs={{0,64},{64,128},{128,192},{192,0},{1,65},{65,129},{129,193},{193,1... | collective-permute-start | bytes 1572872 | tf_op jit(solution)/shard_map/ppermute | solution.py:24
  28.7 23.7 %collective-permute-start.9 = (bf16[64,4096]{1,0:T(8,128)(2,1)}, bf16[64,4096]{1,0:T(8,128)(2,1)S(1)}, u32[]{:S(2)}, u32[]{:S(2)}) collective-permute-start(bf16[64,4096]{1,0:T(8,128)(2,1)} %get-tuple-element.30), channel_id=1, source_target_pairs={{0,128},{64,192},{128,0},{192,64},{1,129},{65,193},{129,1},{193,65... | collective-permute-start | bytes 1572872 | tf_op jit(solution)/shard_map/ppermute | solution.py:24
  30.9 6.7 %collective-permute-start.11 = (bf16[512,128]{1,0:T(8,128)(2,1)}, bf16[512,128]{1,0:T(8,128)(2,1)S(1)}, u32[]{:S(2)}, u32[]{:S(2)}) collective-permute-start(bf16[512,128]{1,0:T(8,128)(2,1)} %copy-done.18), channel_id=1, source_target_pairs={{0,16},{8,24},{16,0},{24,8},{1,17},{9,25},{17,1},{25,9},{2,18},{10... | collective-permute-start | bytes 393224 | tf_op jit(solution)/shard_map/ppermute | solution.py:24
  33.5 6.1 %collective-permute-start.6 = (bf16[704,128]{1,0:T(8,128)(2,1)}, bf16[704,128]{1,0:T(8,128)(2,1)S(1)}, u32[]{:S(2)}, u32[]{:S(2)}) collective-permute-start(bf16[704,128]{1,0:T(8,128)(2,1)} %get-tuple-element.76), channel_id=1, source_target_pairs={{0,8},{8,16},{16,24},{24,0},{1,9},{9,17},{17,25},{25,1},{2,10},{10... | collective-permute-start | bytes 540680 | tf_op jit(solution)/shard_map/ppermute | solution.py:24
  39.7 12.7 %copy-start.2 = (bf16[704,128]{1,0:T(8,128)(2,1)}, bf16[704,128]{1,0:T(8,128)(2,1)S(1)}, u32[]{:S(2)}) copy-start(bf16[704,128]{1,0:T(8,128)(2,1)S(1)} %collective-permute-done.6.rest_2_) | copy-start | bytes 540676
  40.7 16.3 %collective-permute-start.12 = (bf16[2048,128]{1,0:T(8,128)(2,1)}, bf16[2048,128]{1,0:T(8,128)(2,1)}, u32[]{:S(2)}, u32[]{:S(2)}) collective-permute-start(bf16[2048,128]{1,0:T(8,128)(2,1)} %constant_dynamic-slice_fusion.2), channel_id=1, source_target_pairs={{0,32},{32,0},{1,33},{33,1},{2,34},{34,2},{3,35},{35,3},{4,36},{36... | collective-permute-start | bytes 1572872 | tf_op jit(solution)/shard_map/ppermute | solution.py:24
  42.2 24.0 %collective-permute-start = (bf16[192,128]{1,0:T(8,128)(2,1)}, bf16[192,128]{1,0:T(8,128)(2,1)}, u32[]{:S(2)}, u32[]{:S(2)}) collective-permute-start(bf16[192,128]{1,0:T(8,128)(2,1)} %bitcast.8), channel_id=1, source_target_pairs={{0,32},{32,0},{1,33},{33,1},{2,34},{34,2},{3,35},{35,3},{4,36},{36... | collective-permute-start | bytes 147464 | tf_op jit(solution)/shard_map/ppermute | solution.py:24
  48.3 0.8 copy-start.4
  49.1 17.1 %collective-permute-start.1 = (bf16[192,128]{1,0:T(8,128)(2,1)}, bf16[192,128]{1,0:T(8,128)(2,1)}, u32[]{:S(2)}, u32[]{:S(2)}) collective-permute-start(bf16[192,128]{1,0:T(8,128)(2,1)} %bitcast.9), channel_id=1, source_target_pairs={{32,64},{96,128},{160,192},{64,32},{128,96},{192,160},{33,65},{97,... | collective-permute-start | bytes 147464 | tf_op jit(solution)/shard_map/ppermute | solution.py:40
  51.6 0.8 copy-start.6
  52.4 0.8 copy-start.8
  53.2 1.0 copy-start.5
  54.2 1.0 copy-start.7
  55.3 1.0 copy-start.9
  57.0 8.2 %copy-start.19 = (f32[3,8,8,8]{3,2,1,0:T(8,128)S(1)}, f32[3,8,8,8]{3,2,1,0:T(8,128)}, u32[]{:S(2)}) copy-start(f32[3,8,8,8]{3,2,1,0:T(8,128)} %param.8) | copy-start | bytes 18436
  57.0 9.0 %copy-start.20 = (s32[1,1,1,512]{3,2,1,0:T(1,128)S(1)}, s32[1,1,1,512]{3,2,1,0:T(1,128)}, u32[]{:S(2)}) copy-start(s32[1,1,1,512]{3,2,1,0:T(1,128)} %param.12) | copy-start | bytes 6148
  57.0 9.2 %copy-start.3 = (bf16[704,128]{1,0:T(8,128)(2,1)S(1)}, bf16[704,128]{1,0:T(8,128)(2,1)}, u32[]{:S(2)}) copy-start(bf16[704,128]{1,0:T(8,128)(2,1)} %copy-done.2) | copy-start | bytes 540676
  60.0 3.7 %copy-start.17 = (f32[256,128]{1,0:T(8,128)}, f32[256,128]{1,0:T(8,128)S(1)}, u32[]{:S(2)}) copy-start(f32[256,128]{1,0:T(8,128)S(1)} %convolution_add_fusion.1) | copy-start | bytes 393220
  60.7 16.9 %collective-permute-start.13 = (f32[64,128]{1,0:T(8,128)}, f32[64,128]{1,0:T(8,128)S(1)}, u32[]{:S(2)}, u32[]{:S(2)}) collective-permute-start(f32[64,128]{1,0:T(8,128)} %get-tuple-element.72), channel_id=1, source_target_pairs={{0,192},{64,0},{128,64},{192,128},{1,193},{65,1},{129,65},{193,129... | collective-permute-start | bytes 98312 | tf_op jit(solution)/shard_map/ppermute | solution.py:24
  63.7 13.9 %collective-permute-start.15 = (f32[64,128]{1,0:T(8,128)}, f32[64,128]{1,0:T(8,128)S(1)}, u32[]{:S(2)}, u32[]{:S(2)}) collective-permute-start(f32[64,128]{1,0:T(8,128)} %get-tuple-element.73), channel_id=1, source_target_pairs={{0,64},{64,128},{128,192},{192,0},{1,65},{65,129},{129,193},{193,1... | collective-permute-start | bytes 98312 | tf_op jit(solution)/shard_map/ppermute | solution.py:24
  63.7 13.9 %collective-permute-start.14 = (f32[64,128]{1,0:T(8,128)}, f32[64,128]{1,0:T(8,128)}, u32[]{:S(2)}, u32[]{:S(2)}) collective-permute-start(f32[64,128]{1,0:T(8,128)} %get-tuple-element.74), channel_id=1, source_target_pairs={{0,128},{64,192},{128,0},{192,64},{1,129},{65,193},{129,1},{193,65... | collective-permute-start | bytes 98312 | tf_op jit(solution)/shard_map/ppermute | solution.py:24
  66.2 3.4 %copy-start.1 = (bf16[1,1,1,2048,2048]{4,3,2,1,0:T(8,128)(2,1)S(1)}, bf16[1,1,1,2048,2048]{4,3,2,1,0:T(8,128)(2,1)}, u32[]{:S(2)}) copy-start(bf16[1,1,1,2048,2048]{4,3,2,1,0:T(8,128)(2,1)} %param.9) | copy-start | bytes 25165828
  69.6 8.0 %copy-start.13 = (bf16[64,1536]{1,0:T(8,128)(2,1)S(1)}, bf16[64,1536]{1,0:T(8,128)(2,1)}, u32[]{:S(2)}) copy-start(bf16[64,1536]{1,0:T(8,128)(2,1)} %copy-done.12) | copy-start | bytes 589828
  78.8 84.2 %copy-start.10 = (f32[1536,128]{1,0:T(8,128)}, f32[1536,128]{1,0:T(8,128)S(1)}, u32[]{:S(2)}) copy-start(f32[1536,128]{1,0:T(8,128)S(1)} %add.240) | copy-start | bytes 2359300
  79.6 13.8 %collective-permute-start.17 = (bf16[192,128]{1,0:T(8,128)(2,1)S(1)}, bf16[192,128]{1,0:T(8,128)(2,1)S(1)}, u32[]{:S(2)}, u32[]{:S(2)}) collective-permute-start(bf16[192,128]{1,0:T(8,128)(2,1)S(1)} %bitcast.224), channel_id=1, source_target_pairs={{0,32},{32,0},{1,33},{33,1},{2,34},{34,2},{3,35},{35,3},{4,36},{36... | collective-permute-start | bytes 147464 | tf_op jit(solution)/shard_map/ppermute | solution.py:24
  81.0 14.4 %collective-permute-start.16 = (bf16[192,128]{1,0:T(8,128)(2,1)S(1)}, bf16[192,128]{1,0:T(8,128)(2,1)S(1)}, u32[]{:S(2)}, u32[]{:S(2)}) collective-permute-start(bf16[192,128]{1,0:T(8,128)(2,1)S(1)} %bitcast.222), channel_id=1, source_target_pairs={{32,64},{96,128},{160,192},{64,32},{128,96},{192,160},{33,65},{97,... | collective-permute-start | bytes 147464 | tf_op jit(solution)/shard_map/ppermute | solution.py:40
  81.7 13.7 %collective-permute-start.19 = (bf16[192,128]{1,0:T(8,128)(2,1)S(1)}, bf16[192,128]{1,0:T(8,128)(2,1)S(1)}, u32[]{:S(2)}, u32[]{:S(2)}) collective-permute-start(bf16[192,128]{1,0:T(8,128)(2,1)S(1)} %bitcast.240), channel_id=1, source_target_pairs={{8,0},{16,8},{24,16},{9,1},{17,9},{25,17},{10,2},{18,10},{26,18},{... | collective-permute-start | bytes 147464 | tf_op jit(solution)/shard_map/ppermute | solution.py:54
  86.7 8.9 %collective-permute-start.21 = (bf16[192,128]{1,0:T(8,128)(2,1)S(1)}, bf16[192,128]{1,0:T(8,128)(2,1)S(1)}, u32[]{:S(2)}, u32[]{:S(2)}) collective-permute-start(bf16[192,128]{1,0:T(8,128)(2,1)S(1)} %bitcast.233), channel_id=1, source_target_pairs={{1,0},{2,1},{3,2},{4,3},{5,4},{6,5},{7,6},{9,8},{10,9},{11,10},{12... | collective-permute-start | bytes 147464 | tf_op jit(solution)/shard_map/ppermute | solution.py:54
  88.0 7.6 %collective-permute-start.20 = (bf16[192,128]{1,0:T(8,128)(2,1)S(1)}, bf16[192,128]{1,0:T(8,128)(2,1)S(1)}, u32[]{:S(2)}, u32[]{:S(2)}) collective-permute-start(bf16[192,128]{1,0:T(8,128)(2,1)S(1)} %bitcast.231), channel_id=1, source_target_pairs={{0,1},{1,2},{2,3},{3,4},{4,5},{5,6},{6,7},{8,9},{9,10},{10,11},{11... | collective-permute-start | bytes 147464 | tf_op jit(solution)/shard_map/ppermute | solution.py:53
  93.1 6.4 %copy-start.16 = (f32[3,8,8,8]{2,1,0,3:T(8,128)S(1)}, f32[3,8,8,8]{2,1,0,3:T(8,128)}, u32[]{:S(2)}) copy-start(f32[3,8,8,8]{2,1,0,3:T(8,128)} %copy.135) | copy-start | bytes 18436
  93.4 6.0 %collective-permute-start.18 = (bf16[192,128]{1,0:T(8,128)(2,1)S(1)}, bf16[192,128]{1,0:T(8,128)(2,1)S(1)}, u32[]{:S(2)}, u32[]{:S(2)}) collective-permute-start(bf16[192,128]{1,0:T(8,128)(2,1)S(1)} %bitcast.229), channel_id=1, source_target_pairs={{0,8},{8,16},{16,24},{1,9},{9,17},{17,25},{2,10},{10,18},{18,26},{... | collective-permute-start | bytes 147464 | tf_op jit(solution)/shard_map/ppermute | solution.py:53
  99.5 37.2 %slice-start = ((s8[8388608]{0:T(1024)(128)(4,1)}), s8[4194304]{0:T(1024)(128)(4,1)S(1)}, s32[]{:S(2)}) async-start(s8[8388608]{0:T(1024)(128)(4,1)} %bitcast.192), calls=%async_computation.2 | async-start | bytes 8388608
  100.7 36.0 %slice-start.1 = ((s8[8388608]{0:T(1024)(128)(4,1)}), s8[4194304]{0:T(1024)(128)(4,1)S(1)}, s32[]{:S(2)}) async-start(s8[8388608]{0:T(1024)(128)(4,1)} %bitcast.192), calls=%async_computation.3 | async-start | bytes 8388608
  101.2 6.0 %collective-permute-start.24 = (bf16[256,128]{1,0:T(8,128)(2,1)S(1)}, bf16[256,128]{1,0:T(8,128)(2,1)S(1)}, u32[]{:S(2)}, u32[]{:S(2)}) collective-permute-start(bf16[256,128]{1,0:T(8,128)(2,1)S(1)} %get-tuple-element.81), channel_id=1, source_target_pairs={{0,1},{1,2},{2,3},{3,4},{4,5},{5,6},{6,7},{7,0},{8,9},{9,10},{10,1... | collective-permute-start | bytes 196616 | tf_op jit(solution)/shard_map/ppermute | solution.py:24
  102.8 4.4 %collective-permute-start.25 = (bf16[256,128]{1,0:T(8,128)(2,1)S(1)}, bf16[256,128]{1,0:T(8,128)(2,1)S(1)}, u32[]{:S(2)}, u32[]{:S(2)}) collective-permute-start(bf16[256,128]{1,0:T(8,128)(2,1)S(1)} %get-tuple-element.82), channel_id=1, source_target_pairs={{0,7},{1,0},{2,1},{3,2},{4,3},{5,4},{6,5},{7,6},{8,15},{9,8},{10,9... | collective-permute-start | bytes 196616 | tf_op jit(solution)/shard_map/ppermute | solution.py:24
  107.2 7.7 %collective-permute-start.26 = (bf16[192,128]{1,0:T(8,128)(2,1)S(1)}, bf16[192,128]{1,0:T(8,128)(2,1)S(1)}, u32[]{:S(2)}, u32[]{:S(2)}) collective-permute-start(bf16[192,128]{1,0:T(8,128)(2,1)S(1)} %pad_maximum_fusion.9), channel_id=1, source_target_pairs={{0,3},{1,4},{2,5},{3,6},{4,7},{5,0},{6,1},{7,2},{8,11},{9,12},{10,... | collective-permute-start | bytes 147464 | tf_op jit(solution)/shard_map/ppermute | solution.py:24
  110.8 6.6 %collective-permute-start.27 = (bf16[128,128]{1,0:T(8,128)(2,1)S(1)}, bf16[128,128]{1,0:T(8,128)(2,1)S(1)}, u32[]{:S(2)}, u32[]{:S(2)}) collective-permute-start(bf16[128,128]{1,0:T(8,128)(2,1)S(1)} %pad_maximum_fusion.11), channel_id=1, source_target_pairs={{0,5},{1,6},{2,7},{3,0},{4,1},{5,2},{6,3},{7,4},{8,13},{9,14},{10,... | collective-permute-start | bytes 98312 | tf_op jit(solution)/shard_map/ppermute | solution.py:24
  117.5 7.8 %collective-permute-start.29 = (bf16[704,128]{1,0:T(8,128)(2,1)S(1)}, bf16[704,128]{1,0:T(8,128)(2,1)S(1)}, u32[]{:S(2)}, u32[]{:S(2)}) collective-permute-start(bf16[704,128]{1,0:T(8,128)(2,1)S(1)} %get-tuple-element.70), channel_id=1, source_target_pairs={{0,24},{8,0},{16,8},{24,16},{1,25},{9,1},{17,9},{25,17},{2,26},{10... | collective-permute-start | bytes 540680 | tf_op jit(solution)/shard_map/ppermute | solution.py:24
  117.6 7.7 %collective-permute-start.30 = (bf16[512,128]{1,0:T(8,128)(2,1)S(1)}, bf16[512,128]{1,0:T(8,128)(2,1)S(1)}, u32[]{:S(2)}, u32[]{:S(2)}) collective-permute-start(bf16[512,128]{1,0:T(8,128)(2,1)S(1)} %constant_dynamic-slice_fusion.1), channel_id=1, source_target_pairs={{0,16},{8,24},{16,0},{24,8},{1,17},{9,25},{17,1},{25,9},{2,18},{10... | collective-permute-start | bytes 393224 | tf_op jit(solution)/shard_map/ppermute | solution.py:24
  118.9 7.7 %collective-permute-start.28 = (bf16[704,128]{1,0:T(8,128)(2,1)S(1)}, bf16[704,128]{1,0:T(8,128)(2,1)S(1)}, u32[]{:S(2)}, u32[]{:S(2)}) collective-permute-start(bf16[704,128]{1,0:T(8,128)(2,1)S(1)} %get-tuple-element.71), channel_id=1, source_target_pairs={{0,8},{8,16},{16,24},{24,0},{1,9},{9,17},{17,25},{25,1},{2,10},{10... | collective-permute-start | bytes 540680 | tf_op jit(solution)/shard_map/ppermute | solution.py:24
  126.8 2.0 %collective-permute-start.31 = (bf16[2048,128]{1,0:T(8,128)(2,1)S(1)}, bf16[2048,128]{1,0:T(8,128)(2,1)S(1)}, u32[]{:S(2)}, u32[]{:S(2)}) collective-permute-start(bf16[2048,128]{1,0:T(8,128)(2,1)S(1)} %constant_dynamic-slice_fusion), channel_id=1, source_target_pairs={{0,32},{32,0},{1,33},{33,1},{2,34},{34,2},{3,35},{35,3},{4,36},{36... | collective-permute-start | bytes 1572872 | tf_op jit(solution)/shard_map/ppermute | solution.py:24
  127.0 9.7 %collective-permute-start.22 = (bf16[192,128]{1,0:T(8,128)(2,1)S(1)}, bf16[192,128]{1,0:T(8,128)(2,1)S(1)}, u32[]{:S(2)}, u32[]{:S(2)}) collective-permute-start(bf16[192,128]{1,0:T(8,128)(2,1)S(1)} %bitcast.227), channel_id=1, source_target_pairs={{0,32},{32,0},{1,33},{33,1},{2,34},{34,2},{3,35},{35,3},{4,36},{36... | collective-permute-start | bytes 147464 | tf_op jit(solution)/shard_map/ppermute | solution.py:24
  127.6 9.1 %collective-permute-start.23 = (bf16[192,128]{1,0:T(8,128)(2,1)S(1)}, bf16[192,128]{1,0:T(8,128)(2,1)S(1)}, u32[]{:S(2)}, u32[]{:S(2)}) collective-permute-start(bf16[192,128]{1,0:T(8,128)(2,1)S(1)} %bitcast.226), channel_id=1, source_target_pairs={{32,64},{96,128},{160,192},{64,32},{128,96},{192,160},{33,65},{97,... | collective-permute-start | bytes 147464 | tf_op jit(solution)/shard_map/ppermute | solution.py:40
  129.7 14.7 %collective-permute-start.32 = (f32[64,128]{1,0:T(8,128)S(1)}, f32[64,128]{1,0:T(8,128)S(1)}, u32[]{:S(2)}, u32[]{:S(2)}) collective-permute-start(f32[64,128]{1,0:T(8,128)S(1)} %get-tuple-element.67), channel_id=1, source_target_pairs={{0,192},{64,0},{128,64},{192,128},{1,193},{65,1},{129,65},{193,129... | collective-permute-start | bytes 98312 | tf_op jit(solution)/shard_map/ppermute | solution.py:24
  134.9 9.6 %collective-permute-start.34 = (f32[64,128]{1,0:T(8,128)S(1)}, f32[64,128]{1,0:T(8,128)S(1)}, u32[]{:S(2)}, u32[]{:S(2)}) collective-permute-start(f32[64,128]{1,0:T(8,128)S(1)} %get-tuple-element.68), channel_id=1, source_target_pairs={{0,64},{64,128},{128,192},{192,0},{1,65},{65,129},{129,193},{193,1... | collective-permute-start | bytes 98312 | tf_op jit(solution)/shard_map/ppermute | solution.py:24
  134.9 9.6 %collective-permute-start.33 = (f32[64,128]{1,0:T(8,128)S(1)}, f32[64,128]{1,0:T(8,128)S(1)}, u32[]{:S(2)}, u32[]{:S(2)}) collective-permute-start(f32[64,128]{1,0:T(8,128)S(1)} %get-tuple-element.69), channel_id=1, source_target_pairs={{0,128},{64,192},{128,0},{192,64},{1,129},{65,193},{129,1},{193,65... | collective-permute-start | bytes 98312 | tf_op jit(solution)/shard_map/ppermute | solution.py:24
  145.6 11.3 %collective-permute-start.36 = (bf16[192,128]{1,0:T(8,128)(2,1)S(1)}, bf16[192,128]{1,0:T(8,128)(2,1)S(1)}, u32[]{:S(2)}, u32[]{:S(2)}) collective-permute-start(bf16[192,128]{1,0:T(8,128)(2,1)S(1)} %bitcast.225), channel_id=1, source_target_pairs={{0,32},{32,0},{1,33},{33,1},{2,34},{34,2},{3,35},{35,3},{4,36},{36... | collective-permute-start | bytes 147464 | tf_op jit(solution)/shard_map/ppermute | solution.py:24
  145.7 13.4 %collective-permute-start.35 = (bf16[192,128]{1,0:T(8,128)(2,1)S(1)}, bf16[192,128]{1,0:T(8,128)(2,1)S(1)}, u32[]{:S(2)}, u32[]{:S(2)}) collective-permute-start(bf16[192,128]{1,0:T(8,128)(2,1)S(1)} %bitcast.223), channel_id=1, source_target_pairs={{32,64},{96,128},{160,192},{64,32},{128,96},{192,160},{33,65},{97,... | collective-permute-start | bytes 147464 | tf_op jit(solution)/shard_map/ppermute | solution.py:40
  146.4 12.7 %collective-permute-start.38 = (bf16[192,128]{1,0:T(8,128)(2,1)S(1)}, bf16[192,128]{1,0:T(8,128)(2,1)S(1)}, u32[]{:S(2)}, u32[]{:S(2)}) collective-permute-start(bf16[192,128]{1,0:T(8,128)(2,1)S(1)} %bitcast.238), channel_id=1, source_target_pairs={{8,0},{16,8},{24,16},{9,1},{17,9},{25,17},{10,2},{18,10},{26,18},{... | collective-permute-start | bytes 147464 | tf_op jit(solution)/shard_map/ppermute | solution.py:54
  150.2 9.1 %collective-permute-start.40 = (bf16[192,128]{1,0:T(8,128)(2,1)S(1)}, bf16[192,128]{1,0:T(8,128)(2,1)S(1)}, u32[]{:S(2)}, u32[]{:S(2)}) collective-permute-start(bf16[192,128]{1,0:T(8,128)(2,1)S(1)} %bitcast.232), channel_id=1, source_target_pairs={{1,0},{2,1},{3,2},{4,3},{5,4},{6,5},{7,6},{9,8},{10,9},{11,10},{12... | collective-permute-start | bytes 147464 | tf_op jit(solution)/shard_map/ppermute | solution.py:54
  151.5 7.8 %collective-permute-start.39 = (bf16[192,128]{1,0:T(8,128)(2,1)S(1)}, bf16[192,128]{1,0:T(8,128)(2,1)S(1)}, u32[]{:S(2)}, u32[]{:S(2)}) collective-permute-start(bf16[192,128]{1,0:T(8,128)(2,1)S(1)} %bitcast.230), channel_id=1, source_target_pairs={{0,1},{1,2},{2,3},{3,4},{4,5},{5,6},{6,7},{8,9},{9,10},{10,11},{11... | collective-permute-start | bytes 147464 | tf_op jit(solution)/shard_map/ppermute | solution.py:53
  156.6 6.4 %copy-start.15 = (f32[3,8,8,8,128]{4,3,2,1,0:T(8,128)S(1)}, f32[3,8,8,8,128]{4,3,2,1,0:T(8,128)}, u32[]{:S(2)}) copy-start(f32[3,8,8,8,128]{4,3,2,1,0:T(8,128)} %param.7) | copy-start | bytes 2359300
  156.9 6.0 %collective-permute-start.37 = (bf16[192,128]{1,0:T(8,128)(2,1)S(1)}, bf16[192,128]{1,0:T(8,128)(2,1)S(1)}, u32[]{:S(2)}, u32[]{:S(2)}) collective-permute-start(bf16[192,128]{1,0:T(8,128)(2,1)S(1)} %bitcast.228), channel_id=1, source_target_pairs={{0,8},{8,16},{16,24},{1,9},{9,17},{17,25},{2,10},{10,18},{18,26},{... | collective-permute-start | bytes 147464 | tf_op jit(solution)/shard_map/ppermute | solution.py:53
  164.4 28.2 %copy-start.11 = (f32[1536,128]{1,0:T(8,128)S(1)}, f32[1536,128]{1,0:T(8,128)}, u32[]{:S(2)}) copy-start(f32[1536,128]{1,0:T(8,128)} %copy-done.10) | copy-start | bytes 2359300
  (1 other events, 0.8 us)

commit v2 on v0

--- a/solution.py
+++ b/solution.py
@@ -102,7 +102,7 @@
 
 
 def local_kernel(place, order, own, *rest):
-    faces, (factor, out, held, stacked, front, ring, done) = rest[:6], rest[6:]
+    faces, (factor, out, stacked, front, ring) = rest[:6], rest[6:]
     size = stacked.shape[0]
     own_count = own.shape[0]
     tiles = size // TILE
@@ -111,13 +111,6 @@
     def rows(i):
         return pl.ds(pl.multiple_of(i * TILE, TILE), TILE)
 
-    def copy(i, width):
-        return pltpu.make_async_copy(
-            factor.at[rows(i), pl.ds(0, width)], held.at[rows(i), pl.ds(0, width)], done.at[i]
-        )
-
-    for i in range(tiles):
-        copy(i, half if i < tiles // 2 else size).start()
     stacked[:own_count] = own[...]
     inside, across, y_low, y_high, z_low, z_high = faces
     per_part = inside.shape[0] // 3
@@ -149,14 +142,13 @@
     pl.loop(0, order.shape[0] // SOME)(pick)
 
     def ahead(width, i):
-        copy(i, width).wait()
         front[rows(i)] = jnp.dot(
-            held[rows(i), :width], stacked[:width], preferred_element_type=jnp.float32
+            factor[rows(i), :width], stacked[:width], preferred_element_type=jnp.float32
         ).astype(jnp.bfloat16)
 
     def back(skip, j):
         piece = lax.dot_general(
-            front[skip:], held[skip:, rows(j)], contract_first, preferred_element_type=jnp.float32
+            front[skip:], factor[skip:, rows(j)], contract_first, preferred_element_type=jnp.float32
         )
         out[rows(j)] = piece.T
 
@@ -175,15 +167,12 @@
         local_kernel,
         out_shape=jax.ShapeDtypeStruct(own.shape, jnp.float32),
         in_specs=[pl.BlockSpec(memory_space=pltpu.SMEM)]
-        + [vmem] * 8
-        + [pl.BlockSpec(memory_space=pltpu.HBM)],
+        + [vmem] * 9,
         out_specs=vmem,
         scratch_shapes=[
-            pltpu.VMEM((size, size), jnp.bfloat16),
             pltpu.VMEM((size, lanes), jnp.bfloat16),
             pltpu.VMEM((size, lanes), jnp.bfloat16),
             pltpu.VMEM((6 * faces[0].shape[0], lanes), jnp.bfloat16),
-            pltpu.SemaphoreType.DMA((size // TILE,)),
         ],
         compiler_params=pltpu.CompilerParams(vmem_limit_bytes=24 * 1024 * 1024),
         name="local_solve",

time: 200 us -> 198 us (0.990)
  transfers between devices with their start and end apart: 41 -> 41, of which waited for: 14 -> 14; matrix products, arithmetic and copies ran while one was open for 9% -> 9% of each run, Pallas kernels for 10% -> 9%
where the time goes in v2:
time: 198 us; the launch traced here: 197 us
  starting transfers between devices  72.2 us (36%)
  waiting for transfers between devices  38 us (19%)
  blocking collectives  27.3 us (14%)
  local copies, waits for them, and re-layouts  24.3 us (12%)
  Pallas kernels  17.9 us (9%)
  other arithmetic  9.84 us (5%)
  matrix products  5.36 us (3%)
    ppermute x29, starting transfers between devices, shift(): lax.ppermute(value, axis, [(i, (i + step) % count) for i in range(count)])  45.2 us
    ppermute x29, waiting for transfers between devices, shift(): lax.ppermute(value, axis, [(i, (i + step) % count) for i in range(count)])  30.5 us
    all_to_all x2, blocking collectives, everywhere(): partial = jnp.sum(lax.all_to_all(copies, axes, 0, 0, tiled=True), axis=0)  27.3 us
    pallas_call x2, Pallas kernels, local_solve(): pl.pallas_call(local_kernel, out_shape=jax.ShapeDtypeStruct(own.shape, jn...  14.3 us
    ppermute x4, starting transfers between devices, halo(): faces.append(lax.ppermute(last, axis, up))  13.2 us
    unnamed x76, local copies, waits for them, and re-layouts  11.8 us
    ppermute x4, starting transfers between devices, halo(): faces.append(lax.ppermute(first, axis, [(b, a) for a, b in up]))  11.2 us
    ppermute x4, waiting for transfers between devices, halo(): faces.append(lax.ppermute(last, axis, up))  7.45 us
  transfers between devices with their start and end apart: 41, of which 14 were waited for; matrix products, arithmetic and copies ran while one was open for 9% of the time, Pallas kernels for 9%

profile of v2, /device:TPU:8, one launch (start us, length us, event | category | flops | bytes accessed | tf_op | source)
XLA Modules:
  0.0 196.7 jit_solution(3804745968705460134)
XLA Ops:
  0.7 1.4 fusion.8
  2.7 0.6 pad_maximum_fusion.5
  3.4 1.9 collective-permute-start.2
  5.3 3.9 %collective-permute-start.3 = (bf16[256,128]{1,0:T(8,128)(2,1)}, bf16[256,128]{1,0:T(8,128)(2,1)S(1)}, u32[]{:S(2)}, u32[]{:S(2)}) collective-permute-start(bf16[256,128]{1,0:T(8,128)(2,1)} %get-tuple-element.83), channel_id=1, source_target_pairs={{0,7},{1,0},{2,1},{3,2},{4,3},{5,4},{6,5},{7,6},{8,15},{9,8},{10,9... | collective-permute-start | bytes 196616 | tf_op jit(solution)/shard_map/ppermute | solution.py:24
  9.3 0.8 fusion.54
  10.0 1.5 copy.140
  11.5 0.6 copy.139
  12.2 4.7 %collective-permute-start.4 = (bf16[192,128]{1,0:T(8,128)(2,1)S(1)}, bf16[192,128]{1,0:T(8,128)(2,1)S(1)}, u32[]{:S(2)}, u32[]{:S(2)}) collective-permute-start(bf16[192,128]{1,0:T(8,128)(2,1)S(1)} %pad_maximum_fusion.8), channel_id=1, source_target_pairs={{0,3},{1,4},{2,5},{3,6},{4,7},{5,0},{6,1},{7,2},{8,11},{9,12},{10,... | collective-permute-start | bytes 147464 | tf_op jit(solution)/shard_map/ppermute | solution.py:24
  17.3 2.6 %collective-permute-done.4 = bf16[192,128]{1,0:T(8,128)(2,1)S(1)} collective-permute-done((bf16[192,128]{1,0:T(8,128)(2,1)S(1)}, bf16[192,128]{1,0:T(8,128)(2,1)S(1)}, u32[]{:S(2)}, u32[]{:S(2)}) %collective-permute-start.4) | collective-permute-done | bytes 49184 | tf_op jit(solution)/shard_map/ppermute | solution.py:24
  26.3 1.6 constant_dynamic-slice_fusion.6
  27.8 1.7 pad_maximum_fusion
  30.0 1.2 constant_dynamic-slice_fusion.3
  31.2 2.8 %collective-permute-start.10 = (bf16[64,4096]{1,0:T(8,128)(2,1)}, bf16[64,4096]{1,0:T(8,128)(2,1)S(1)}, u32[]{:S(2)}, u32[]{:S(2)}) collective-permute-start(bf16[64,4096]{1,0:T(8,128)(2,1)} %get-tuple-element.27), channel_id=1, source_target_pairs={{0,192},{64,0},{128,64},{192,128},{1,193},{65,1},{129,65},{193,129... | collective-permute-start | bytes 1572872 | tf_op jit(solution)/shard_map/ppermute | solution.py:24
  33.9 0.8 collective-permute-start.9
  34.7 0.9 collective-permute-start.8
  35.6 2.6 %collective-permute-start.11 = (bf16[512,128]{1,0:T(8,128)(2,1)}, bf16[512,128]{1,0:T(8,128)(2,1)S(1)}, u32[]{:S(2)}, u32[]{:S(2)}) collective-permute-start(bf16[512,128]{1,0:T(8,128)(2,1)} %constant_dynamic-slice_fusion.6), channel_id=1, source_target_pairs={{0,16},{8,24},{16,0},{24,8},{1,17},{9,25},{17,1},{25,9},{2,18},{10... | collective-permute-start | bytes 393224 | tf_op jit(solution)/shard_map/ppermute | solution.py:24
  38.2 1.9 collective-permute-start.6
  40.1 2.2 %collective-permute-done.11 = bf16[512,128]{1,0:T(8,128)(2,1)S(1)} collective-permute-done((bf16[512,128]{1,0:T(8,128)(2,1)}, bf16[512,128]{1,0:T(8,128)(2,1)S(1)}, u32[]{:S(2)}, u32[]{:S(2)}) %collective-permute-start.11) | collective-permute-done | bytes 131104 | tf_op jit(solution)/shard_map/ppermute | solution.py:24
  42.3 2.0 %collective-permute-done.6.rest_2_ = bf16[704,128]{1,0:T(8,128)(2,1)S(1)} collective-permute-done((bf16[704,128]{1,0:T(8,128)(2,1)}, bf16[704,128]{1,0:T(8,128)(2,1)S(1)}, u32[]{:S(2)}, u32[]{:S(2)}) %collective-permute-start.6) | collective-permute-done | bytes 180256 | tf_op jit(solution)/shard_map/ppermute | solution.py:24
  44.4 0.9 constant_dynamic-update-slice_fusion.12
  45.4 0.9 constant_dynamic-update-slice_fusion.10
  46.5 0.8 broadcast_select_fusion.10
  49.6 5.1 %collective-permute-done.10.refs_3_ = bf16[64,4096]{1,0:T(8,128)(2,1)S(1)} collective-permute-done((bf16[64,4096]{1,0:T(8,128)(2,1)}, bf16[64,4096]{1,0:T(8,128)(2,1)S(1)}, u32[]{:S(2)}, u32[]{:S(2)}) %collective-permute-start.10) | collective-permute-done | bytes 524320 | tf_op jit(solution)/shard_map/ppermute | solution.py:24
  54.7 0.7 collective-permute-start.1
  55.4 3.0 %collective-permute-done.8.refs_1_ = bf16[64,4096]{1,0:T(8,128)(2,1)} collective-permute-done((bf16[64,4096]{1,0:T(8,128)(2,1)}, bf16[64,4096]{1,0:T(8,128)(2,1)}, u32[]{:S(2)}, u32[]{:S(2)}) %collective-permute-start.8) | collective-permute-done | bytes 524320 | tf_op jit(solution)/shard_map/ppermute | solution.py:24
  58.4 3.7 %stack.82 = (bf16[256,2048]{1,0:T(8,128)(2,1)}, bf16[256,2048]{1,0:T(8,128)(2,1)}) custom-call(s32[2]{0:T(128)} %pad_add_fusion.place, bf16[64,16384]{1,0:T(8,128)(2,1)} %refs_0_.1, bf16[64,4096]{1,0:T(8,128)(2,1)} %collective-permute-done.8.refs_1_, bf16[64,4096]{1,0:T(8,128)(2,1)} %copy-done.10, bf16[64,4096]{1,0:T(8,128)(2,1)} %copy-done.9), custom_call_target="tpu_custom_call" | custom-call | tf_op jit(solution)/shard_map/stack/pallas_call | solution.py:198
  62.1 1.7 fusion.58
  63.7 1.6 convolution_add_fusion.1
  65.4 2.7 %collective-permute-start.13 = (f32[64,128]{1,0:T(8,128)S(1)}, f32[64,128]{1,0:T(8,128)S(1)}, u32[]{:S(2)}, u32[]{:S(2)}) collective-permute-start(f32[64,128]{1,0:T(8,128)S(1)} %get-tuple-element.71), channel_id=1, source_target_pairs={{0,192},{64,0},{128,64},{192,128},{1,193},{65,1},{129,65},{193,129... | collective-permute-start | bytes 98312 | tf_op jit(solution)/shard_map/ppermute | solution.py:24
  68.1 1.7 collective-permute-start.14
  70.3 3.4 %copy-done.1 = bf16[1,1,1,2048,2048]{4,3,2,1,0:T(8,128)(2,1)S(1)} copy-done((bf16[1,1,1,2048,2048]{4,3,2,1,0:T(8,128)(2,1)S(1)}, bf16[1,1,1,2048,2048]{4,3,2,1,0:T(8,128)(2,1)}, u32[]{:S(2)}) %copy-start.1) | copy-done | bytes 8388632
  73.7 7.1 %local_solve.2 = f32[1536,128]{1,0:T(8,128)S(1)} custom-call(s32[5]{0:T(128)S(1)} %stack.69.place, s32[512,1]{1,0:T(8,128)S(1)} %copy.141.order, bf16[1536,128]{1,0:T(8,128)(2,1)S(1)} %bitcast.197, bf16[192,128]{1,0:T(8,128)(2,1)S(1)} %collective-permute-done.rest_0_, bf16[192,128]{1,0:T(8,128)(2,1)S(1)} %collective-permute-done.1.rest_1_, ...), custom_call_target="tpu_custom_call" | custom-call | tf_op jit(solution)/shard_map/local_solve/pallas_call | solution.py:166
  82.1 1.1 collective-permute-start.17
  83.2 0.7 collective-permute-start.16
  83.9 4.9 %collective-permute-start.19 = (bf16[192,128]{1,0:T(8,128)(2,1)S(1)}, bf16[192,128]{1,0:T(8,128)(2,1)S(1)}, u32[]{:S(2)}, u32[]{:S(2)}) collective-permute-start(bf16[192,128]{1,0:T(8,128)(2,1)S(1)} %bitcast.241), channel_id=1, source_target_pairs={{8,0},{16,8},{24,16},{9,1},{17,9},{25,17},{10,2},{18,10},{26,18},{... | collective-permute-start | bytes 147464 | tf_op jit(solution)/shard_map/ppermute | solution.py:54
  88.8 1.3 collective-permute-start.21
  90.1 4.5 %collective-permute-start.20 = (bf16[192,128]{1,0:T(8,128)(2,1)S(1)}, bf16[192,128]{1,0:T(8,128)(2,1)S(1)}, u32[]{:S(2)}, u32[]{:S(2)}) collective-permute-start(bf16[192,128]{1,0:T(8,128)(2,1)S(1)} %bitcast.232), channel_id=1, source_target_pairs={{0,1},{1,2},{2,3},{3,4},{4,5},{5,6},{6,7},{8,9},{9,10},{10,11},{11... | collective-permute-start | bytes 147464 | tf_op jit(solution)/shard_map/ppermute | solution.py:53
  95.6 1.9 collective-permute-start.18
  97.8 3.8 %collective-permute-done.18 = bf16[192,128]{1,0:T(8,128)(2,1)S(1)} collective-permute-done((bf16[192,128]{1,0:T(8,128)(2,1)S(1)}, bf16[192,128]{1,0:T(8,128)(2,1)S(1)}, u32[]{:S(2)}, u32[]{:S(2)}) %collective-permute-start.18) | collective-permute-done | bytes 49184 | tf_op jit(solution)/shard_map/ppermute | solution.py:53
  101.7 0.7 fusion.9
  103.4 1.6 collective-permute-start.24
  105.0 1.7 collective-permute-start.25
  106.9 2.5 %collective-permute-done.24.rest_4_ = bf16[256,128]{1,0:T(8,128)(2,1)S(1)} collective-permute-done((bf16[256,128]{1,0:T(8,128)(2,1)S(1)}, bf16[256,128]{1,0:T(8,128)(2,1)S(1)}, u32[]{:S(2)}, u32[]{:S(2)}) %collective-permute-start.24) | collective-permute-done | bytes 65568 | tf_op jit(solution)/shard_map/ppermute | solution.py:24
  109.5 4.7 %collective-permute-start.26 = (bf16[192,128]{1,0:T(8,128)(2,1)S(1)}, bf16[192,128]{1,0:T(8,128)(2,1)S(1)}, u32[]{:S(2)}, u32[]{:S(2)}) collective-permute-start(bf16[192,128]{1,0:T(8,128)(2,1)S(1)} %pad_maximum_fusion.9), channel_id=1, source_target_pairs={{0,3},{1,4},{2,5},{3,6},{4,7},{5,0},{6,1},{7,2},{8,11},{9,12},{10,... | collective-permute-start | bytes 147464 | tf_op jit(solution)/shard_map/ppermute | solution.py:24
  114.6 2.4 %collective-permute-done.26 = bf16[192,128]{1,0:T(8,128)(2,1)S(1)} collective-permute-done((bf16[192,128]{1,0:T(8,128)(2,1)S(1)}, bf16[192,128]{1,0:T(8,128)(2,1)S(1)}, u32[]{:S(2)}, u32[]{:S(2)}) %collective-permute-start.26) | collective-permute-done | bytes 49184 | tf_op jit(solution)/shard_map/ppermute | solution.py:24
  117.0 3.4 %collective-permute-done.27 = bf16[128,128]{1,0:T(8,128)(2,1)S(1)} collective-permute-done((bf16[128,128]{1,0:T(8,128)(2,1)S(1)}, bf16[128,128]{1,0:T(8,128)(2,1)S(1)}, u32[]{:S(2)}, u32[]{:S(2)}) %collective-permute-start.27) | collective-permute-done | bytes 32800 | tf_op jit(solution)/shard_map/ppermute | solution.py:24
  120.7 1.3 collective-permute-start.30
  122.0 1.4 collective-permute-start.28
  123.4 4.6 %collective-permute-done.29.rest_3_ = bf16[704,128]{1,0:T(8,128)(2,1)S(1)} collective-permute-done((bf16[704,128]{1,0:T(8,128)(2,1)S(1)}, bf16[704,128]{1,0:T(8,128)(2,1)S(1)}, u32[]{:S(2)}, u32[]{:S(2)}) %collective-permute-start.29) | collective-permute-done | bytes 180256 | tf_op jit(solution)/shard_map/ppermute | solution.py:24
  128.0 1.8 collective-permute-done.28.rest_2_
  130.7 0.7 collective-permute-start.23
  132.9 4.9 %collective-permute-start.32 = (f32[64,128]{1,0:T(8,128)S(1)}, f32[64,128]{1,0:T(8,128)S(1)}, u32[]{:S(2)}, u32[]{:S(2)}) collective-permute-start(f32[64,128]{1,0:T(8,128)S(1)} %get-tuple-element.66), channel_id=1, source_target_pairs={{0,192},{64,0},{128,64},{192,128},{1,193},{65,1},{129,65},{193,129... | collective-permute-start | bytes 98312 | tf_op jit(solution)/shard_map/ppermute | solution.py:24
  137.8 1.8 collective-permute-start.33
  139.7 7.1 %local_solve.3 = f32[1536,128]{1,0:T(8,128)S(1)} custom-call(s32[5]{0:T(128)S(1)} %stack.69.place, s32[512,1]{1,0:T(8,128)S(1)} %copy.141.order, bf16[1536,128]{1,0:T(8,128)(2,1)S(1)} %get-tuple-element.25.own, bf16[192,128]{1,0:T(8,128)(2,1)S(1)} %collective-permute-done.22.rest_0_, bf16[192,128]{1,0:T(8,128)(2,1)S(1)} %collective-permute-done.23.rest_1_, ...), custom_call_target="tpu_custom_call" | custom-call | tf_op jit(solution)/shard_map/local_solve/pallas_call | solution.py:166
  148.2 0.7 collective-permute-start.35
  148.9 3.7 %collective-permute-start.38 = (bf16[192,128]{1,0:T(8,128)(2,1)S(1)}, bf16[192,128]{1,0:T(8,128)(2,1)S(1)}, u32[]{:S(2)}, u32[]{:S(2)}) collective-permute-start(bf16[192,128]{1,0:T(8,128)(2,1)S(1)} %bitcast.239), channel_id=1, source_target_pairs={{8,0},{16,8},{24,16},{9,1},{17,9},{25,17},{10,2},{18,10},{26,18},{... | collective-permute-start | bytes 147464 | tf_op jit(solution)/shard_map/ppermute | solution.py:54
  152.6 1.3 collective-permute-start.40
  153.9 4.6 %collective-permute-start.39 = (bf16[192,128]{1,0:T(8,128)(2,1)S(1)}, bf16[192,128]{1,0:T(8,128)(2,1)S(1)}, u32[]{:S(2)}, u32[]{:S(2)}) collective-permute-start(bf16[192,128]{1,0:T(8,128)(2,1)S(1)} %bitcast.231), channel_id=1, source_target_pairs={{0,1},{1,2},{2,3},{3,4},{4,5},{5,6},{6,7},{8,9},{9,10},{10,11},{11... | collective-permute-start | bytes 147464 | tf_op jit(solution)/shard_map/ppermute | solution.py:53
  159.4 2.1 %collective-permute-start.37 = (bf16[192,128]{1,0:T(8,128)(2,1)S(1)}, bf16[192,128]{1,0:T(8,128)(2,1)S(1)}, u32[]{:S(2)}, u32[]{:S(2)}) collective-permute-start(bf16[192,128]{1,0:T(8,128)(2,1)S(1)} %bitcast.229), channel_id=1, source_target_pairs={{0,8},{8,16},{16,24},{1,9},{9,17},{17,25},{2,10},{10,18},{18,26},{... | collective-permute-start | bytes 147464 | tf_op jit(solution)/shard_map/ppermute | solution.py:53
  161.8 3.6 %collective-permute-done.37 = bf16[192,128]{1,0:T(8,128)(2,1)S(1)} collective-permute-done((bf16[192,128]{1,0:T(8,128)(2,1)S(1)}, bf16[192,128]{1,0:T(8,128)(2,1)S(1)}, u32[]{:S(2)}, u32[]{:S(2)}) %collective-permute-start.37) | collective-permute-done | bytes 49184 | tf_op jit(solution)/shard_map/ppermute | solution.py:53
  165.5 1.4 multiply_reduce_fusion.2
  167.7 13.2 %all_to_all.10 = f32[16,6,128]{2,1,0:T(8,128)S(1)} all-to-all(f32[16,6,128]{2,1,0:T(8,128)S(1)} %broadcast_in_dim.4), channel_id=1, replica_groups=mesh['gx_0'=4,'gx_1'=2,'gy_0'=2,'gy_1'=2,'gz'=8] {'gx_0','gx_1','gy_1'}, dimensions={0} | all-to-all | bytes 98304 | tf_op jit(solution)/shard_map/all_to_all | solution.py:267
  181.0 14.1 %all_to_all.11 = f32[16,6,128]{2,1,0:T(8,128)S(1)} all-to-all(f32[16,6,128]{2,1,0:T(8,128)S(1)} %broadcast_in_dim.5), channel_id=1, replica_groups=mesh['gx_0'=4,'gx_1'=2,'gy_0'=2,'gy_1'=2,'gz'=8] {'gy_0','gz'}, dimensions={0} | all-to-all | bytes 98304 | tf_op jit(solution)/shard_map/all_to_all | solution.py:267
  195.6 1.0 multiply_add_fusion
  (206 shorter events, 21.2 us)
Async XLA Ops:
  0.6 1.7 copy-start
  0.6 1.7 copy-start.13
  2.0 27.5 %copy-start.7 = (bf16[3,8,8,8,128]{4,2,1,0,3:T(8,128)(2,1)}, bf16[3,8,8,8,128]{4,2,1,0,3:T(8,128)(2,1)S(1)}, u32[]{:S(2)}) copy-start(bf16[3,8,8,8,128]{4,2,1,0,3:T(8,128)(2,1)S(1)} %fusion.8) | copy-start | bytes 1179652
  2.0 28.0 %copy-start.2 = (bf16[64,16384]{1,0:T(8,128)(2,1)S(1)}, bf16[64,16384]{1,0:T(8,128)(2,1)}, u32[]{:S(2)}) copy-start(bf16[64,16384]{1,0:T(8,128)(2,1)} %refs_0_.1) | copy-start | bytes 6291460
  2.5 28.6 %copy-start.3 = (bf16[64,1536]{1,0:T(8,128)(2,1)}, bf16[64,1536]{1,0:T(8,128)(2,1)S(1)}, u32[]{:S(2)}) copy-start(bf16[64,1536]{1,0:T(8,128)(2,1)S(1)} %convolution_convert_fusion) | copy-start | bytes 589828
  3.4 8.8 %collective-permute-start.2 = (bf16[256,128]{1,0:T(8,128)(2,1)}, bf16[256,128]{1,0:T(8,128)(2,1)S(1)}, u32[]{:S(2)}, u32[]{:S(2)}) collective-permute-start(bf16[256,128]{1,0:T(8,128)(2,1)} %get-tuple-element.82), channel_id=1, source_target_pairs={{0,1},{1,2},{2,3},{3,4},{4,5},{5,6},{6,7},{7,0},{8,9},{9,10},{10,1... | collective-permute-start | bytes 196616 | tf_op jit(solution)/shard_map/ppermute | solution.py:24
  5.3 6.9 %collective-permute-start.3 = (bf16[256,128]{1,0:T(8,128)(2,1)}, bf16[256,128]{1,0:T(8,128)(2,1)S(1)}, u32[]{:S(2)}, u32[]{:S(2)}) collective-permute-start(bf16[256,128]{1,0:T(8,128)(2,1)} %get-tuple-element.83), channel_id=1, source_target_pairs={{0,7},{1,0},{2,1},{3,2},{4,3},{5,4},{6,5},{7,6},{8,15},{9,8},{10,9... | collective-permute-start | bytes 196616 | tf_op jit(solution)/shard_map/ppermute | solution.py:24
  12.2 7.7 %collective-permute-start.4 = (bf16[192,128]{1,0:T(8,128)(2,1)S(1)}, bf16[192,128]{1,0:T(8,128)(2,1)S(1)}, u32[]{:S(2)}, u32[]{:S(2)}) collective-permute-start(bf16[192,128]{1,0:T(8,128)(2,1)S(1)} %pad_maximum_fusion.8), channel_id=1, source_target_pairs={{0,3},{1,4},{2,5},{3,6},{4,7},{5,0},{6,1},{7,2},{8,11},{9,12},{10,... | collective-permute-start | bytes 147464 | tf_op jit(solution)/shard_map/ppermute | solution.py:24
  16.9 5.7 %collective-permute-start.5 = (bf16[128,128]{1,0:T(8,128)(2,1)S(1)}, bf16[128,128]{1,0:T(8,128)(2,1)S(1)}, u32[]{:S(2)}, u32[]{:S(2)}) collective-permute-start(bf16[128,128]{1,0:T(8,128)(2,1)S(1)} %pad_maximum_fusion.10), channel_id=1, source_target_pairs={{0,5},{1,6},{2,7},{3,0},{4,1},{5,2},{6,3},{7,4},{8,13},{9,14},{10,... | collective-permute-start | bytes 98312 | tf_op jit(solution)/shard_map/ppermute | solution.py:24
  29.5 8.7 %collective-permute-start.7 = (bf16[704,128]{1,0:T(8,128)(2,1)}, bf16[704,128]{1,0:T(8,128)(2,1)S(1)}, u32[]{:S(2)}, u32[]{:S(2)}) collective-permute-start(bf16[704,128]{1,0:T(8,128)(2,1)} %get-tuple-element.74), channel_id=1, source_target_pairs={{0,24},{8,0},{16,8},{24,16},{1,25},{9,1},{17,9},{25,17},{2,26},{10... | collective-permute-start | bytes 540680 | tf_op jit(solution)/shard_map/ppermute | solution.py:24
  31.2 23.5 %collective-permute-start.10 = (bf16[64,4096]{1,0:T(8,128)(2,1)}, bf16[64,4096]{1,0:T(8,128)(2,1)S(1)}, u32[]{:S(2)}, u32[]{:S(2)}) collective-permute-start(bf16[64,4096]{1,0:T(8,128)(2,1)} %get-tuple-element.27), channel_id=1, source_target_pairs={{0,192},{64,0},{128,64},{192,128},{1,193},{65,1},{129,65},{193,129... | collective-permute-start | bytes 1572872 | tf_op jit(solution)/shard_map/ppermute | solution.py:24
  33.9 21.4 %collective-permute-start.9 = (bf16[64,4096]{1,0:T(8,128)(2,1)}, bf16[64,4096]{1,0:T(8,128)(2,1)S(1)}, u32[]{:S(2)}, u32[]{:S(2)}) collective-permute-start(bf16[64,4096]{1,0:T(8,128)(2,1)} %get-tuple-element.28), channel_id=1, source_target_pairs={{0,128},{64,192},{128,0},{192,64},{1,129},{65,193},{129,1},{193,65... | collective-permute-start | bytes 1572872 | tf_op jit(solution)/shard_map/ppermute | solution.py:24
  34.7 23.7 %collective-permute-start.8 = (bf16[64,4096]{1,0:T(8,128)(2,1)}, bf16[64,4096]{1,0:T(8,128)(2,1)}, u32[]{:S(2)}, u32[]{:S(2)}) collective-permute-start(bf16[64,4096]{1,0:T(8,128)(2,1)} %get-tuple-element.29), channel_id=1, source_target_pairs={{0,64},{64,128},{128,192},{192,0},{1,65},{65,129},{129,193},{193,1... | collective-permute-start | bytes 1572872 | tf_op jit(solution)/shard_map/ppermute | solution.py:24
  35.6 6.7 %collective-permute-start.11 = (bf16[512,128]{1,0:T(8,128)(2,1)}, bf16[512,128]{1,0:T(8,128)(2,1)S(1)}, u32[]{:S(2)}, u32[]{:S(2)}) collective-permute-start(bf16[512,128]{1,0:T(8,128)(2,1)} %constant_dynamic-slice_fusion.6), channel_id=1, source_target_pairs={{0,16},{8,24},{16,0},{24,8},{1,17},{9,25},{17,1},{25,9},{2,18},{10... | collective-permute-start | bytes 393224 | tf_op jit(solution)/shard_map/ppermute | solution.py:24
  38.2 6.1 %collective-permute-start.6 = (bf16[704,128]{1,0:T(8,128)(2,1)}, bf16[704,128]{1,0:T(8,128)(2,1)S(1)}, u32[]{:S(2)}, u32[]{:S(2)}) collective-permute-start(bf16[704,128]{1,0:T(8,128)(2,1)} %get-tuple-element.75), channel_id=1, source_target_pairs={{0,8},{8,16},{16,24},{24,0},{1,9},{9,17},{17,25},{25,1},{2,10},{10... | collective-permute-start | bytes 540680 | tf_op jit(solution)/shard_map/ppermute | solution.py:24
  46.4 15.7 %collective-permute-start.12 = (bf16[2048,128]{1,0:T(8,128)(2,1)S(1)}, bf16[2048,128]{1,0:T(8,128)(2,1)S(1)}, u32[]{:S(2)}, u32[]{:S(2)}) collective-permute-start(bf16[2048,128]{1,0:T(8,128)(2,1)S(1)} %constant_dynamic-slice_fusion.2), channel_id=1, source_target_pairs={{0,32},{32,0},{1,33},{33,1},{2,34},{34,2},{3,35},{35,3},{4,36},{36... | collective-permute-start | bytes 1572872 | tf_op jit(solution)/shard_map/ppermute | solution.py:24
  47.9 22.4 %collective-permute-start = (bf16[192,128]{1,0:T(8,128)(2,1)}, bf16[192,128]{1,0:T(8,128)(2,1)S(1)}, u32[]{:S(2)}, u32[]{:S(2)}) collective-permute-start(bf16[192,128]{1,0:T(8,128)(2,1)} %bitcast.8), channel_id=1, source_target_pairs={{0,32},{32,0},{1,33},{33,1},{2,34},{34,2},{3,35},{35,3},{4,36},{36... | collective-permute-start | bytes 147464 | tf_op jit(solution)/shard_map/ppermute | solution.py:24
  54.7 3.7 %copy-start.9 = (bf16[64,4096]{1,0:T(8,128)(2,1)}, bf16[64,4096]{1,0:T(8,128)(2,1)S(1)}, u32[]{:S(2)}) copy-start(bf16[64,4096]{1,0:T(8,128)(2,1)S(1)} %collective-permute-done.10.refs_3_) | copy-start | bytes 1572868
  54.7 15.6 %collective-permute-start.1 = (bf16[192,128]{1,0:T(8,128)(2,1)}, bf16[192,128]{1,0:T(8,128)(2,1)S(1)}, u32[]{:S(2)}, u32[]{:S(2)}) collective-permute-start(bf16[192,128]{1,0:T(8,128)(2,1)} %bitcast.9), channel_id=1, source_target_pairs={{32,64},{96,128},{160,192},{64,32},{128,96},{192,160},{33,65},{97,... | collective-permute-start | bytes 147464 | tf_op jit(solution)/shard_map/ppermute | solution.py:40
  55.4 3.0 %copy-start.10 = (bf16[64,4096]{1,0:T(8,128)(2,1)}, bf16[64,4096]{1,0:T(8,128)(2,1)S(1)}, u32[]{:S(2)}) copy-start(bf16[64,4096]{1,0:T(8,128)(2,1)S(1)} %collective-permute-done.9.refs_2_) | copy-start | bytes 1572868
  62.0 7.8 %copy-start.11 = (f32[3,8,8,8]{3,2,1,0:T(8,128)S(1)}, f32[3,8,8,8]{3,2,1,0:T(8,128)}, u32[]{:S(2)}) copy-start(f32[3,8,8,8]{3,2,1,0:T(8,128)} %param.8) | copy-start | bytes 18436
  62.1 8.0 %copy-start.12 = (s32[1,1,1,512]{3,2,1,0:T(1,128)S(1)}, s32[1,1,1,512]{3,2,1,0:T(1,128)}, u32[]{:S(2)}) copy-start(s32[1,1,1,512]{3,2,1,0:T(1,128)} %param.12) | copy-start | bytes 6148
  65.4 15.4 %collective-permute-start.13 = (f32[64,128]{1,0:T(8,128)S(1)}, f32[64,128]{1,0:T(8,128)S(1)}, u32[]{:S(2)}, u32[]{:S(2)}) collective-permute-start(f32[64,128]{1,0:T(8,128)S(1)} %get-tuple-element.71), channel_id=1, source_target_pairs={{0,192},{64,0},{128,64},{192,128},{1,193},{65,1},{129,65},{193,129... | collective-permute-start | bytes 98312 | tf_op jit(solution)/shard_map/ppermute | solution.py:24
  68.1 12.8 %collective-permute-start.15 = (f32[64,128]{1,0:T(8,128)S(1)}, f32[64,128]{1,0:T(8,128)S(1)}, u32[]{:S(2)}, u32[]{:S(2)}) collective-permute-start(f32[64,128]{1,0:T(8,128)S(1)} %get-tuple-element.72), channel_id=1, source_target_pairs={{0,64},{64,128},{128,192},{192,0},{1,65},{65,129},{129,193},{193,1... | collective-permute-start | bytes 98312 | tf_op jit(solution)/shard_map/ppermute | solution.py:24
  68.1 12.8 %collective-permute-start.14 = (f32[64,128]{1,0:T(8,128)S(1)}, f32[64,128]{1,0:T(8,128)S(1)}, u32[]{:S(2)}, u32[]{:S(2)}) collective-permute-start(f32[64,128]{1,0:T(8,128)S(1)} %get-tuple-element.73), channel_id=1, source_target_pairs={{0,128},{64,192},{128,0},{192,64},{1,129},{65,193},{129,1},{193,65... | collective-permute-start | bytes 98312 | tf_op jit(solution)/shard_map/ppermute | solution.py:24
  70.3 3.4 %copy-start.1 = (bf16[1,1,1,2048,2048]{4,3,2,1,0:T(8,128)(2,1)S(1)}, bf16[1,1,1,2048,2048]{4,3,2,1,0:T(8,128)(2,1)}, u32[]{:S(2)}) copy-start(bf16[1,1,1,2048,2048]{4,3,2,1,0:T(8,128)(2,1)} %param.9) | copy-start | bytes 25165828
  73.7 7.2 %copy-start.4 = (bf16[64,1536]{1,0:T(8,128)(2,1)S(1)}, bf16[64,1536]{1,0:T(8,128)(2,1)}, u32[]{:S(2)}) copy-start(bf16[64,1536]{1,0:T(8,128)(2,1)} %copy-done.3) | copy-start | bytes 589828
  82.1 13.5 %collective-permute-start.17 = (bf16[192,128]{1,0:T(8,128)(2,1)S(1)}, bf16[192,128]{1,0:T(8,128)(2,1)S(1)}, u32[]{:S(2)}, u32[]{:S(2)}) collective-permute-start(bf16[192,128]{1,0:T(8,128)(2,1)S(1)} %bitcast.225), channel_id=1, source_target_pairs={{0,32},{32,0},{1,33},{33,1},{2,34},{34,2},{3,35},{35,3},{4,36},{36... | collective-permute-start | bytes 147464 | tf_op jit(solution)/shard_map/ppermute | solution.py:24
  83.2 14.4 %collective-permute-start.16 = (bf16[192,128]{1,0:T(8,128)(2,1)S(1)}, bf16[192,128]{1,0:T(8,128)(2,1)S(1)}, u32[]{:S(2)}, u32[]{:S(2)}) collective-permute-start(bf16[192,128]{1,0:T(8,128)(2,1)S(1)} %bitcast.223), channel_id=1, source_target_pairs={{32,64},{96,128},{160,192},{64,32},{128,96},{192,160},{33,65},{97,... | collective-permute-start | bytes 147464 | tf_op jit(solution)/shard_map/ppermute | solution.py:40
  83.9 13.7 %collective-permute-start.19 = (bf16[192,128]{1,0:T(8,128)(2,1)S(1)}, bf16[192,128]{1,0:T(8,128)(2,1)S(1)}, u32[]{:S(2)}, u32[]{:S(2)}) collective-permute-start(bf16[192,128]{1,0:T(8,128)(2,1)S(1)} %bitcast.241), channel_id=1, source_target_pairs={{8,0},{16,8},{24,16},{9,1},{17,9},{25,17},{10,2},{18,10},{26,18},{... | collective-permute-start | bytes 147464 | tf_op jit(solution)/shard_map/ppermute | solution.py:54
  88.8 8.9 %collective-permute-start.21 = (bf16[192,128]{1,0:T(8,128)(2,1)S(1)}, bf16[192,128]{1,0:T(8,128)(2,1)S(1)}, u32[]{:S(2)}, u32[]{:S(2)}) collective-permute-start(bf16[192,128]{1,0:T(8,128)(2,1)S(1)} %bitcast.234), channel_id=1, source_target_pairs={{1,0},{2,1},{3,2},{4,3},{5,4},{6,5},{7,6},{9,8},{10,9},{11,10},{12... | collective-permute-start | bytes 147464 | tf_op jit(solution)/shard_map/ppermute | solution.py:54
  90.1 7.6 %collective-permute-start.20 = (bf16[192,128]{1,0:T(8,128)(2,1)S(1)}, bf16[192,128]{1,0:T(8,128)(2,1)S(1)}, u32[]{:S(2)}, u32[]{:S(2)}) collective-permute-start(bf16[192,128]{1,0:T(8,128)(2,1)S(1)} %bitcast.232), channel_id=1, source_target_pairs={{0,1},{1,2},{2,3},{3,4},{4,5},{5,6},{6,7},{8,9},{9,10},{10,11},{11... | collective-permute-start | bytes 147464 | tf_op jit(solution)/shard_map/ppermute | solution.py:53
  95.6 6.0 %collective-permute-start.18 = (bf16[192,128]{1,0:T(8,128)(2,1)S(1)}, bf16[192,128]{1,0:T(8,128)(2,1)S(1)}, u32[]{:S(2)}, u32[]{:S(2)}) collective-permute-start(bf16[192,128]{1,0:T(8,128)(2,1)S(1)} %bitcast.230), channel_id=1, source_target_pairs={{0,8},{8,16},{16,24},{1,9},{9,17},{17,25},{2,10},{10,18},{18,26},{... | collective-permute-start | bytes 147464 | tf_op jit(solution)/shard_map/ppermute | solution.py:53
  101.7 38.0 %slice-start = ((s8[8388608]{0:T(1024)(128)(4,1)}), s8[4194304]{0:T(1024)(128)(4,1)S(1)}, s32[]{:S(2)}) async-start(s8[8388608]{0:T(1024)(128)(4,1)} %bitcast.193), calls=%async_computation.2 | async-start | bytes 8388608
  102.9 36.8 %slice-start.1 = ((s8[8388608]{0:T(1024)(128)(4,1)}), s8[4194304]{0:T(1024)(128)(4,1)S(1)}, s32[]{:S(2)}) async-start(s8[8388608]{0:T(1024)(128)(4,1)} %bitcast.193), calls=%async_computation.3 | async-start | bytes 8388608
  103.4 6.0 %collective-permute-start.24 = (bf16[256,128]{1,0:T(8,128)(2,1)S(1)}, bf16[256,128]{1,0:T(8,128)(2,1)S(1)}, u32[]{:S(2)}, u32[]{:S(2)}) collective-permute-start(bf16[256,128]{1,0:T(8,128)(2,1)S(1)} %get-tuple-element.80), channel_id=1, source_target_pairs={{0,1},{1,2},{2,3},{3,4},{4,5},{5,6},{6,7},{7,0},{8,9},{9,10},{10,1... | collective-permute-start | bytes 196616 | tf_op jit(solution)/shard_map/ppermute | solution.py:24
  105.0 4.5 %collective-permute-start.25 = (bf16[256,128]{1,0:T(8,128)(2,1)S(1)}, bf16[256,128]{1,0:T(8,128)(2,1)S(1)}, u32[]{:S(2)}, u32[]{:S(2)}) collective-permute-start(bf16[256,128]{1,0:T(8,128)(2,1)S(1)} %get-tuple-element.81), channel_id=1, source_target_pairs={{0,7},{1,0},{2,1},{3,2},{4,3},{5,4},{6,5},{7,6},{8,15},{9,8},{10,9... | collective-permute-start | bytes 196616 | tf_op jit(solution)/shard_map/ppermute | solution.py:24
  109.5 7.5 %collective-permute-start.26 = (bf16[192,128]{1,0:T(8,128)(2,1)S(1)}, bf16[192,128]{1,0:T(8,128)(2,1)S(1)}, u32[]{:S(2)}, u32[]{:S(2)}) collective-permute-start(bf16[192,128]{1,0:T(8,128)(2,1)S(1)} %pad_maximum_fusion.9), channel_id=1, source_target_pairs={{0,3},{1,4},{2,5},{3,6},{4,7},{5,0},{6,1},{7,2},{8,11},{9,12},{10,... | collective-permute-start | bytes 147464 | tf_op jit(solution)/shard_map/ppermute | solution.py:24
  114.2 6.2 %collective-permute-start.27 = (bf16[128,128]{1,0:T(8,128)(2,1)S(1)}, bf16[128,128]{1,0:T(8,128)(2,1)S(1)}, u32[]{:S(2)}, u32[]{:S(2)}) collective-permute-start(bf16[128,128]{1,0:T(8,128)(2,1)S(1)} %pad_maximum_fusion.11), channel_id=1, source_target_pairs={{0,5},{1,6},{2,7},{3,0},{4,1},{5,2},{6,3},{7,4},{8,13},{9,14},{10,... | collective-permute-start | bytes 98312 | tf_op jit(solution)/shard_map/ppermute | solution.py:24
  120.5 11.5 %copy-start.6 = (bf16[256,2048]{1,0:T(8,128)(2,1)S(1)}, bf16[256,2048]{1,0:T(8,128)(2,1)}, u32[]{:S(2)}) copy-start(bf16[256,2048]{1,0:T(8,128)(2,1)} %get-tuple-element.5) | copy-start | bytes 3145732
  120.6 7.4 %collective-permute-start.29 = (bf16[704,128]{1,0:T(8,128)(2,1)S(1)}, bf16[704,128]{1,0:T(8,128)(2,1)S(1)}, u32[]{:S(2)}, u32[]{:S(2)}) collective-permute-start(bf16[704,128]{1,0:T(8,128)(2,1)S(1)} %get-tuple-element.69), channel_id=1, source_target_pairs={{0,24},{8,0},{16,8},{24,16},{1,25},{9,1},{17,9},{25,17},{2,26},{10... | collective-permute-start | bytes 540680 | tf_op jit(solution)/shard_map/ppermute | solution.py:24
  120.7 7.3 %collective-permute-start.30 = (bf16[512,128]{1,0:T(8,128)(2,1)S(1)}, bf16[512,128]{1,0:T(8,128)(2,1)S(1)}, u32[]{:S(2)}, u32[]{:S(2)}) collective-permute-start(bf16[512,128]{1,0:T(8,128)(2,1)S(1)} %constant_dynamic-slice_fusion.1), channel_id=1, source_target_pairs={{0,16},{8,24},{16,0},{24,8},{1,17},{9,25},{17,1},{25,9},{2,18},{10... | collective-permute-start | bytes 393224 | tf_op jit(solution)/shard_map/ppermute | solution.py:24
  122.0 7.7 %collective-permute-start.28 = (bf16[704,128]{1,0:T(8,128)(2,1)S(1)}, bf16[704,128]{1,0:T(8,128)(2,1)S(1)}, u32[]{:S(2)}, u32[]{:S(2)}) collective-permute-start(bf16[704,128]{1,0:T(8,128)(2,1)S(1)} %get-tuple-element.70), channel_id=1, source_target_pairs={{0,8},{8,16},{16,24},{24,0},{1,9},{9,17},{17,25},{25,1},{2,10},{10... | collective-permute-start | bytes 540680 | tf_op jit(solution)/shard_map/ppermute | solution.py:24
  129.8 2.6 %copy-start.5 = (bf16[256,2048]{1,0:T(8,128)(2,1)S(1)}, bf16[256,2048]{1,0:T(8,128)(2,1)}, u32[]{:S(2)}) copy-start(bf16[256,2048]{1,0:T(8,128)(2,1)} %get-tuple-element.4) | copy-start | bytes 3145732
  130.0 2.0 %collective-permute-start.31 = (bf16[2048,128]{1,0:T(8,128)(2,1)S(1)}, bf16[2048,128]{1,0:T(8,128)(2,1)S(1)}, u32[]{:S(2)}, u32[]{:S(2)}) collective-permute-start(bf16[2048,128]{1,0:T(8,128)(2,1)S(1)} %constant_dynamic-slice_fusion), channel_id=1, source_target_pairs={{0,32},{32,0},{1,33},{33,1},{2,34},{34,2},{3,35},{35,3},{4,36},{36... | collective-permute-start | bytes 1572872 | tf_op jit(solution)/shard_map/ppermute | solution.py:24
  130.1 9.5 %collective-permute-start.22 = (bf16[192,128]{1,0:T(8,128)(2,1)S(1)}, bf16[192,128]{1,0:T(8,128)(2,1)S(1)}, u32[]{:S(2)}, u32[]{:S(2)}) collective-permute-start(bf16[192,128]{1,0:T(8,128)(2,1)S(1)} %bitcast.228), channel_id=1, source_target_pairs={{0,32},{32,0},{1,33},{33,1},{2,34},{34,2},{3,35},{35,3},{4,36},{36... | collective-permute-start | bytes 147464 | tf_op jit(solution)/shard_map/ppermute | solution.py:24
  130.7 8.9 %collective-permute-start.23 = (bf16[192,128]{1,0:T(8,128)(2,1)S(1)}, bf16[192,128]{1,0:T(8,128)(2,1)S(1)}, u32[]{:S(2)}, u32[]{:S(2)}) collective-permute-start(bf16[192,128]{1,0:T(8,128)(2,1)S(1)} %bitcast.227), channel_id=1, source_target_pairs={{32,64},{96,128},{160,192},{64,32},{128,96},{192,160},{33,65},{97,... | collective-permute-start | bytes 147464 | tf_op jit(solution)/shard_map/ppermute | solution.py:40
  132.9 14.0 %collective-permute-start.32 = (f32[64,128]{1,0:T(8,128)S(1)}, f32[64,128]{1,0:T(8,128)S(1)}, u32[]{:S(2)}, u32[]{:S(2)}) collective-permute-start(f32[64,128]{1,0:T(8,128)S(1)} %get-tuple-element.66), channel_id=1, source_target_pairs={{0,192},{64,0},{128,64},{192,128},{1,193},{65,1},{129,65},{193,129... | collective-permute-start | bytes 98312 | tf_op jit(solution)/shard_map/ppermute | solution.py:24
  137.8 9.0 %collective-permute-start.34 = (f32[64,128]{1,0:T(8,128)S(1)}, f32[64,128]{1,0:T(8,128)S(1)}, u32[]{:S(2)}, u32[]{:S(2)}) collective-permute-start(f32[64,128]{1,0:T(8,128)S(1)} %get-tuple-element.67), channel_id=1, source_target_pairs={{0,64},{64,128},{128,192},{192,0},{1,65},{65,129},{129,193},{193,1... | collective-permute-start | bytes 98312 | tf_op jit(solution)/shard_map/ppermute | solution.py:24
  137.8 9.0 %collective-permute-start.33 = (f32[64,128]{1,0:T(8,128)S(1)}, f32[64,128]{1,0:T(8,128)S(1)}, u32[]{:S(2)}, u32[]{:S(2)}) collective-permute-start(f32[64,128]{1,0:T(8,128)S(1)} %get-tuple-element.68), channel_id=1, source_target_pairs={{0,128},{64,192},{128,0},{192,64},{1,129},{65,193},{129,1},{193,65... | collective-permute-start | bytes 98312 | tf_op jit(solution)/shard_map/ppermute | solution.py:24
  148.1 11.3 %collective-permute-start.36 = (bf16[192,128]{1,0:T(8,128)(2,1)S(1)}, bf16[192,128]{1,0:T(8,128)(2,1)S(1)}, u32[]{:S(2)}, u32[]{:S(2)}) collective-permute-start(bf16[192,128]{1,0:T(8,128)(2,1)S(1)} %bitcast.226), channel_id=1, source_target_pairs={{0,32},{32,0},{1,33},{33,1},{2,34},{34,2},{3,35},{35,3},{4,36},{36... | collective-permute-start | bytes 147464 | tf_op jit(solution)/shard_map/ppermute | solution.py:24
  148.2 13.4 %collective-permute-start.35 = (bf16[192,128]{1,0:T(8,128)(2,1)S(1)}, bf16[192,128]{1,0:T(8,128)(2,1)S(1)}, u32[]{:S(2)}, u32[]{:S(2)}) collective-permute-start(bf16[192,128]{1,0:T(8,128)(2,1)S(1)} %bitcast.224), channel_id=1, source_target_pairs={{32,64},{96,128},{160,192},{64,32},{128,96},{192,160},{33,65},{97,... | collective-permute-start | bytes 147464 | tf_op jit(solution)/shard_map/ppermute | solution.py:40
  148.9 12.7 %collective-permute-start.38 = (bf16[192,128]{1,0:T(8,128)(2,1)S(1)}, bf16[192,128]{1,0:T(8,128)(2,1)S(1)}, u32[]{:S(2)}, u32[]{:S(2)}) collective-permute-start(bf16[192,128]{1,0:T(8,128)(2,1)S(1)} %bitcast.239), channel_id=1, source_target_pairs={{8,0},{16,8},{24,16},{9,1},{17,9},{25,17},{10,2},{18,10},{26,18},{... | collective-permute-start | bytes 147464 | tf_op jit(solution)/shard_map/ppermute | solution.py:54
  152.6 9.1 %collective-permute-start.40 = (bf16[192,128]{1,0:T(8,128)(2,1)S(1)}, bf16[192,128]{1,0:T(8,128)(2,1)S(1)}, u32[]{:S(2)}, u32[]{:S(2)}) collective-permute-start(bf16[192,128]{1,0:T(8,128)(2,1)S(1)} %bitcast.233), channel_id=1, source_target_pairs={{1,0},{2,1},{3,2},{4,3},{5,4},{6,5},{7,6},{9,8},{10,9},{11,10},{12... | collective-permute-start | bytes 147464 | tf_op jit(solution)/shard_map/ppermute | solution.py:54
  153.9 7.8 %collective-permute-start.39 = (bf16[192,128]{1,0:T(8,128)(2,1)S(1)}, bf16[192,128]{1,0:T(8,128)(2,1)S(1)}, u32[]{:S(2)}, u32[]{:S(2)}) collective-permute-start(bf16[192,128]{1,0:T(8,128)(2,1)S(1)} %bitcast.231), channel_id=1, source_target_pairs={{0,1},{1,2},{2,3},{3,4},{4,5},{5,6},{6,7},{8,9},{9,10},{10,11},{11... | collective-permute-start | bytes 147464 | tf_op jit(solution)/shard_map/ppermute | solution.py:53
  159.1 6.4 %copy-start.8 = (f32[3,8,8,8,128]{4,3,2,1,0:T(8,128)S(1)}, f32[3,8,8,8,128]{4,3,2,1,0:T(8,128)}, u32[]{:S(2)}) copy-start(f32[3,8,8,8,128]{4,3,2,1,0:T(8,128)} %param.7) | copy-start | bytes 2359300
  159.4 6.0 %collective-permute-start.37 = (bf16[192,128]{1,0:T(8,128)(2,1)S(1)}, bf16[192,128]{1,0:T(8,128)(2,1)S(1)}, u32[]{:S(2)}, u32[]{:S(2)}) collective-permute-start(bf16[192,128]{1,0:T(8,128)(2,1)S(1)} %bitcast.229), channel_id=1, source_target_pairs={{0,8},{8,16},{16,24},{1,9},{9,17},{17,25},{2,10},{10,18},{18,26},{... | collective-permute-start | bytes 147464 | tf_op jit(solution)/shard_map/ppermute | solution.py:53
